TPU v7x, 32 devices: a whole 2x2x4 slice. The times are simulated.
32 devices in a mesh: dom: 8 (over y, x, core), grp: 4 (over z).
Axes of the slice: x: 2, y: 2, z: 4, core: 2. Of those that a mesh axis runs over, the one named last changes fastest.
Arguments:
- embeddings: float32 [4, 4096, 512], P('grp', 'dom'), may hold values from -18 to 18
- ada_state: float32 [4, 4096], P('grp', 'dom'), may hold values from 0.05 to 1
- relations: float32 [4, 512, 512], replicated, may hold values from -0.25 to 0.25
- plan: int32 [2], replicated, may hold values from 1 to 7, as said below
- src_rows: int32 [4, 8, 2, 512], P('grp', 'dom'), may hold values from 0 to 511
- dst_rows: int32 [4, 8, 2, 512], P('grp', 'dom'), may hold values from 0 to 511
- rel_ids: int32 [4, 8, 2, 512], P('grp', 'dom'), may hold values from 0 to 3
Outputs:
- new_embeddings: float32 [4, 4096, 512], P('grp', 'dom')
- new_state: float32 [4, 4096], P('grp', 'dom')
- rel_grad: float32 [4, 512, 512], replicated
- mean_loss: float32 [], replicated
Inputs may be any that keep to these rules, and one draw needn't show every extreme that they name: `plan`: the 2 values are distinct; 7 occurs.
All inputs are finite; a program needn't handle non-finite values.
Results may differ from a plain program's by a relative error of at most 0.02.
Values may be sent and summed in bfloat16 or wider, within the bound.
No kernel may reach another device: no remote copies, remote signals or barrier semaphores. Data moves between devices by JAX's collectives and lax.ppermute only.
A program may use at most 64 MiB of HBM per device.

v0:
```python
import jax
import jax.numpy as jnp
from jax import lax
from jax.sharding import PartitionSpec as P

EDGES = 512
ROUNDS = 2


LEARN_RATE = 0.1
EPSILON = 1e-08


def from_partner(block, axis, apart):
    count = lax.axis_size(axis)
    route = []
    for low in range(count):
        high = low | 1 << apart
        if high != low and high < count:
            route += [(low, high), (high, low)]
    return lax.ppermute(block, axis, route)


def project_queries(own_rows, src_idx, rel_idx, rel_b):
    src_b = own_rows[src_idx].astype(jnp.bfloat16)
    projected = jnp.einsum("ed,kdf->kef", src_b, rel_b, preferred_element_type=jnp.float32)
    onehot = (rel_idx[None, :] == jnp.arange(rel_b.shape[0], dtype=jnp.int32)[:, None]).astype(
        jnp.float32
    )
    queries = jnp.sum(onehot[:, :, None] * projected, axis=0).astype(jnp.bfloat16)
    return (src_b, queries, onehot)


def score_block(queries, block_b, dst_idx):
    scores = jnp.dot(queries, block_b.T, preferred_element_type=jnp.float32)
    row_max = jnp.max(scores, axis=1, keepdims=True)
    exp_scores = jnp.exp(scores - row_max)
    row_total = jnp.sum(exp_scores, axis=1, keepdims=True)
    targets = (dst_idx[:, None] == jnp.arange(block_b.shape[0], dtype=jnp.int32)[None, :]).astype(
        jnp.float32
    )
    edge_loss = row_max[:, 0] + jnp.log(row_total[:, 0]) - jnp.sum(scores * targets, axis=1)
    deltas = (exp_scores / row_total - targets).astype(jnp.bfloat16)
    dquery = jnp.dot(deltas, block_b, preferred_element_type=jnp.float32).astype(jnp.bfloat16)
    dblock = lax.dot_general(
        deltas, queries, (((0,), (0,)), ((), ())), preferred_element_type=jnp.float32
    ).astype(jnp.bfloat16)
    return (jnp.sum(edge_loss), dquery, dblock)


def apply_back(dquery, src_b, onehot, rel_b, src_idx, row_count):
    back_proj = jnp.einsum("ef,kdf->ked", dquery, rel_b, preferred_element_type=jnp.float32)
    src_grad = jnp.sum(onehot[:, :, None] * back_proj, axis=0)
    gradient = jnp.zeros((row_count, src_grad.shape[1]), jnp.float32).at[src_idx].add(src_grad)
    masked = (onehot[:, :, None] * dquery.astype(jnp.float32)).astype(jnp.bfloat16)
    rel_part = jnp.einsum("ed,kef->kdf", src_b, masked, preferred_element_type=jnp.float32)
    return (gradient, rel_part)


def body(embeddings, ada_state, relations, plan, src_rows, dst_rows, rel_ids):
    own_rows = embeddings[0]
    row_state = ada_state[0]
    rel_b = relations.astype(jnp.bfloat16)
    row_count = own_rows.shape[0]
    bit_count = lax.axis_size("dom").bit_length() - 1
    loss_sum = jnp.zeros((), jnp.float32)
    rel_sum = jnp.zeros(relations.shape, jnp.float32)
    for round_no in range(ROUNDS):
        round_mask = plan[round_no]
        bit_flags = [
            jnp.bitwise_and(jnp.right_shift(round_mask, bit_no), 1) == 1
            for bit_no in range(bit_count)
        ]
        src_idx = src_rows[0, 0, round_no]
        dst_idx = dst_rows[0, 0, round_no]
        rel_idx = rel_ids[0, 0, round_no]
        src_b, queries, onehot = project_queries(own_rows, src_idx, rel_idx, rel_b)
        own_b = own_rows.astype(jnp.bfloat16)
        remote = own_b
        for bit_no in range(bit_count):
            arrived = from_partner(remote, "dom", bit_no)
            remote = jnp.where(bit_flags[bit_no], arrived, remote)
        edge_loss, dquery, dblock = score_block(queries, remote, dst_idx)
        for bit_no in range(bit_count):
            arrived = from_partner(dblock, "dom", bit_no)
            dblock = jnp.where(bit_flags[bit_no], arrived, dblock)
        gradient, rel_part = apply_back(dquery, src_b, onehot, rel_b, src_idx, row_count)
        gradient = gradient + dblock.astype(jnp.float32)
        row_state = row_state + jnp.mean(gradient * gradient, axis=-1)
        own_rows = own_rows - LEARN_RATE * gradient / (jnp.sqrt(row_state)[:, None] + EPSILON)
        loss_sum = loss_sum + edge_loss
        rel_sum = rel_sum + rel_part
    rel_total, loss_total = lax.psum((rel_sum, loss_sum), ("dom", "grp"))
    mean_loss = loss_total / (lax.axis_size("dom") * lax.axis_size("grp") * ROUNDS * EDGES)
    return (own_rows[None], row_state[None], rel_total, mean_loss)


def solution(mesh):
    return jax.shard_map(
        body,
        mesh=mesh,
        in_specs=(
            P("grp", "dom", None),
            P("grp", "dom"),
            P(),
            P(),
            P("grp", "dom", None, None),
            P("grp", "dom", None, None),
            P("grp", "dom", None, None),
        ),
        out_specs=(P("grp", "dom", None), P("grp", "dom"), P(), P()),
        check_vma=False,
    )
```

profile of v0, /device:TPU:0, one launch (start us, length us, event | category | flops | bytes accessed | tf_op | source)
XLA Modules:
  0.0 281.9 jit_solution(15805332072350460709)
XLA Ops:
  7.2 0.0 all-reduce.2.cloned.1.call-start
  7.2 1.4 bitcast_convert_fusion
  8.6 0.6 collective-permute-start
  9.2 1.3 fusion.33
  12.4 3.8 %convert_element_type.79 = bf16[4,512,512]{2,1,0:T(8,128)(2,1)} convert(f32[4,512,512]{2,1,0:T(8,128)} %param.9) | non-fusion elementwise | flops 1048576 | bytes 6291456 | tf_op jit(solution)/shard_map/convert_element_type | solution.py:63
  16.2 0.1 broadcast_select_fusion.6
  16.3 2.6 collective-permute-start.1
  18.9 1.6 gather_fusion
  20.5 11.0 %collective-permute-done.1 = bf16[512,512]{1,0:T(8,128)(2,1)S(1)} collective-permute-done((bf16[512,512]{1,0:T(8,128)(2,1)S(1)}, bf16[512,512]{1,0:T(8,128)(2,1)S(1)}, u32[]{:S(2)}, u32[]{:S(2)}) %collective-permute-start.1) | collective-permute-done | bytes 524320 | tf_op jit(solution)/shard_map/ppermute | solution.py:21
  31.5 0.1 broadcast_select_fusion.8
  31.5 1.8 collective-permute-start.2
  33.4 2.9 %fusion.3 = bf16[512,512]{1,0:T(8,128)(2,1)S(1)} fusion(bf16[4,512,512]{2,1,0:T(8,128)(2,1)} %convert_element_type.79, f32[4,512]{1,0:T(4,128)S(1)} %fusion.27, bf16[512,512]{1,0:T(8,128)(2,1)S(1)} %gather_fusion), kind=kOutput, calls=%fused_computation.11 | convolution fusion | flops 1075576832 | bytes 3153920 | tf_op jit(solution)/shard_map/ed,kdf->kef/dot_general | solution.py:26
  36.3 9.1 %collective-permute-done.2 = bf16[512,512]{1,0:T(8,128)(2,1)S(1)} collective-permute-done((bf16[512,512]{1,0:T(8,128)(2,1)S(1)}, bf16[512,512]{1,0:T(8,128)(2,1)S(1)}, u32[]{:S(2)}, u32[]{:S(2)}) %collective-permute-start.2) | collective-permute-done | bytes 524320 | tf_op jit(solution)/shard_map/ppermute | solution.py:21
  45.3 0.5 fusion.34
  45.8 0.3 select_reduce_fusion.1
  46.1 0.5 convolution_convert_fusion.3
  46.6 0.1 collective-permute-start.3
  46.7 1.9 collective-permute-done.3
  48.6 0.1 broadcast_select_fusion.5
  48.6 1.5 collective-permute-start.4
  50.2 12.5 %collective-permute-done.4 = bf16[512,512]{1,0:T(8,128)(2,1)S(1)} collective-permute-done((bf16[512,512]{1,0:T(8,128)(2,1)S(1)}, bf16[512,512]{1,0:T(8,128)(2,1)S(1)}, u32[]{:S(2)}, u32[]{:S(2)}) %collective-permute-start.4) | collective-permute-done | bytes 524320 | tf_op jit(solution)/shard_map/ppermute | solution.py:21
  62.7 0.1 broadcast_select_fusion.7
  62.7 1.6 collective-permute-start.5
  64.3 1.6 fusion.36
  65.8 2.3 fusion.2
  68.2 7.7 %collective-permute-done.5 = bf16[512,512]{1,0:T(8,128)(2,1)S(1)} collective-permute-done((bf16[512,512]{1,0:T(8,128)(2,1)S(1)}, bf16[512,512]{1,0:T(8,128)(2,1)S(1)}, u32[]{:S(2)}, u32[]{:S(2)}) %collective-permute-start.5) | collective-permute-done | bytes 524320 | tf_op jit(solution)/shard_map/ppermute | solution.py:21
  75.9 0.1 select_convert_fusion.1
  76.0 4.8 %scatter_fusion = f32[512,512]{1,0:T(8,128)S(1)} fusion(f32[512,512]{1,0:T(8,128)S(1)} %select_convert_fusion.1, s32[512]{0:T(512)S(1)} %bitcast.73, f32[512,512]{1,0:T(8,128)} %fusion.2), kind=kCustom, calls=%fused_computation.2 | custom fusion | flops 262144 | bytes 3147776 | tf_op jit(solution)/shard_map/scatter-add | solution.py:54
  80.9 0.1 multiply_reduce_fusion.1
  81.0 0.2 fusion.30
  81.3 0.1 collective-permute-start.6
  82.2 1.1 collective-permute-done.6
  83.3 0.1 broadcast_select_fusion.1
  83.3 1.5 collective-permute-start.7
  86.2 11.2 %collective-permute-done.7 = bf16[512,512]{1,0:T(8,128)(2,1)S(1)} collective-permute-done((bf16[512,512]{1,0:T(8,128)(2,1)S(1)}, bf16[512,512]{1,0:T(8,128)(2,1)S(1)}, u32[]{:S(2)}, u32[]{:S(2)}) %collective-permute-start.7) | collective-permute-done | bytes 524320 | tf_op jit(solution)/shard_map/ppermute | solution.py:21
  97.4 0.9 broadcast_select_fusion.3
  98.2 1.5 collective-permute-start.8
  99.7 2.2 gather_fusion.1
  102.0 2.3 fusion.1
  104.3 7.3 %collective-permute-done.8 = bf16[512,512]{1,0:T(8,128)(2,1)} collective-permute-done((bf16[512,512]{1,0:T(8,128)(2,1)}, bf16[512,512]{1,0:T(8,128)(2,1)}, u32[]{:S(2)}, u32[]{:S(2)}) %collective-permute-start.8) | collective-permute-done | bytes 524320 | tf_op jit(solution)/shard_map/ppermute | solution.py:21
  111.7 1.6 fusion.35
  113.3 0.3 select_reduce_fusion
  113.6 0.5 convolution_convert_fusion.1
  114.1 0.1 collective-permute-start.9
  114.2 1.6 fusion.4
  115.8 2.5 fusion.37
  118.3 0.8 broadcast_select_fusion
  119.2 1.5 collective-permute-start.10
  120.6 3.7 %add_bitcast_fusion = f32[4,512,512]{1,2,0:T(8,128)} fusion(f32[4,512,512]{2,1,0:T(8,128)S(1)} %fusion.4, f32[512,512]{1,0:T(8,128)S(1)} %get-tuple-element.35, f32[4,512]{1,0:T(4,128)S(1)} %fusion.28, bf16[512,512]{1,0:T(8,128)(2,1)S(1)} %copy-done.3), kind=kOutput, calls=%fused_computation.12 | convolution fusion | flops 1076887552 | bytes 9969664 | tf_op jit(solution)/shard_map/ed,kef->kdf/dot_general | solution.py:56
  124.4 0.0 all-reduce.2.cloned.1.call-update
  124.4 11.3 %collective-permute-done.10 = bf16[512,512]{1,0:T(8,128)(2,1)} collective-permute-done((bf16[512,512]{1,0:T(8,128)(2,1)}, bf16[512,512]{1,0:T(8,128)(2,1)}, u32[]{:S(2)}, u32[]{:S(2)}) %collective-permute-start.10) | collective-permute-done | bytes 524320 | tf_op jit(solution)/shard_map/ppermute | solution.py:21
  135.7 1.9 broadcast_select_fusion.2
  137.6 1.4 collective-permute-start.11
  139.0 0.6 subtract_reduce_fusion.1
  139.6 0.6 subtract_reduce_fusion
  141.5 47.6 %psum.15 = f32[]{:T(128)} all-reduce(f32[]{:T(128)S(6)} %add.100), channel_id=1, replica_groups=mesh['dom'=8,'grp'=4] {'dom','grp'}, use_global_device_ids=true, to_apply=%region_17.18 | all-reduce | flops 1 | bytes 8 | tf_op jit(solution)/shard_map/psum | solution.py:93
  189.8 3.4 %fusion = f32[512,512]{1,0:T(8,128)} fusion(bf16[4,512,512]{2,1,0:T(8,128)(2,1)S(1)} %copy-done.2, f32[4,512]{1,0:T(4,128)S(1)} %fusion.28, bf16[512,512]{1,0:T(8,128)(2,1)} %get-tuple-element.36), kind=kOutput, calls=%fused_computation.5 | convolution fusion | flops 1075576832 | bytes 3678208 | tf_op jit(solution)/shard_map/ef,kdf->ked/dot_general | solution.py:52
  193.2 1.1 select_convert_fusion
  194.3 4.7 %scatter_fusion.1 = f32[512,512]{1,0:T(8,128)S(1)} fusion(f32[512,512]{1,0:T(8,128)S(1)} %select_convert_fusion, s32[512]{0:T(512)S(1)} %bitcast.71, f32[512,512]{1,0:T(8,128)} %fusion), kind=kCustom, calls=%fused_computation.3 | custom fusion | flops 262144 | bytes 3147776 | tf_op jit(solution)/shard_map/scatter-add | solution.py:54
  199.0 0.2 multiply_reduce_fusion
  199.1 0.6 add_add_fusion
  199.7 1.2 subtract_bitcast_fusion
  200.9 67.8 %all-reduce.2.cloned.1.call-done = f32[4,512,512]{1,2,0:T(8,128)} async-done(((f32[4,512,512]{1,2,0:T(8,128)}), f32[4,512,512]{1,2,0:T(8,128)}) %all-reduce.2.cloned.1.call-update) | async-done | bytes 4194320 | tf_op jit(solution)/shard_map/psum | solution.py:93
  268.7 5.2 %copy.16 = f32[4,512,512]{2,1,0:T(8,128)} copy(f32[4,512,512]{1,2,0:T(8,128)} %all-reduce.2.cloned.1.call-done) | data formatting | bytes 8388608
  (34 shorter events, 0.1 us)
Async XLA Ops:
  7.2 9.1 %copy-start = (f32[1,512,512]{2,1,0:T(8,128)S(1)}, f32[1,512,512]{2,1,0:T(8,128)}, u32[]{:S(2)}) copy-start(f32[1,512,512]{2,1,0:T(8,128)} %param.7) | copy-start | bytes 3145732
  7.2 9.0 %copy-start.7 = (s32[1,1,2,512]{3,2,1,0:T(2,128)S(1)}, s32[1,1,2,512]{3,2,1,0:T(2,128)}, u32[]{:S(2)}) copy-start(s32[1,1,2,512]{3,2,1,0:T(2,128)} %param.11) | copy-start | bytes 12292
  7.2 261.5 %all-reduce.2.cloned.1.call-start = ((), (), s32[]{:S(2)}) async-start(), calls=%async_computation | async-start | bytes 8388608 | tf_op jit(solution)/shard_map/psum | solution.py:93
  8.6 7.6 %collective-permute-start = (bf16[512,512]{1,0:T(8,128)(2,1)S(1)}, bf16[512,512]{1,0:T(8,128)(2,1)S(1)}, u32[]{:S(2)}, u32[]{:S(2)}) collective-permute-start(bf16[512,512]{1,0:T(8,128)(2,1)S(1)} %bitcast_convert_fusion), channel_id=1, source_target_pairs={{0,4},{4,0},{8,12},{12,8},{16,20},{20,16},{24,28},{28,24},{1,5},{5... | collective-permute-start | bytes 1572872 | tf_op jit(solution)/shard_map/ppermute | solution.py:21
  16.2 4.3 %copy-start.8 = (s32[1,1,2,512]{3,2,1,0:T(2,128)S(1)}, s32[1,1,2,512]{3,2,1,0:T(2,128)}, u32[]{:S(2)}) copy-start(s32[1,1,2,512]{3,2,1,0:T(2,128)} %param.13) | copy-start | bytes 12292
  16.2 17.1 %copy-start.9 = (s32[1,1,2,512]{3,2,1,0:T(2,128)S(1)}, s32[1,1,2,512]{3,2,1,0:T(2,128)}, u32[]{:S(2)}) copy-start(s32[1,1,2,512]{3,2,1,0:T(2,128)} %param.12) | copy-start | bytes 12292
  16.3 15.1 %collective-permute-start.1 = (bf16[512,512]{1,0:T(8,128)(2,1)S(1)}, bf16[512,512]{1,0:T(8,128)(2,1)S(1)}, u32[]{:S(2)}, u32[]{:S(2)}) collective-permute-start(bf16[512,512]{1,0:T(8,128)(2,1)S(1)} %broadcast_select_fusion.6), channel_id=1, source_target_pairs={{0,8},{8,0},{4,12},{12,4},{16,24},{24,16},{20,28},{28,20},{1,9},{9... | collective-permute-start | bytes 1572872 | tf_op jit(solution)/shard_map/ppermute | solution.py:21
  20.5 25.3 %copy-start.4 = (bf16[512,512]{1,0:T(8,128)(2,1)}, bf16[512,512]{1,0:T(8,128)(2,1)S(1)}, u32[]{:S(2)}) copy-start(bf16[512,512]{1,0:T(8,128)(2,1)S(1)} %gather_fusion) | copy-start | bytes 1572868
  31.5 13.8 %collective-permute-start.2 = (bf16[512,512]{1,0:T(8,128)(2,1)S(1)}, bf16[512,512]{1,0:T(8,128)(2,1)S(1)}, u32[]{:S(2)}, u32[]{:S(2)}) collective-permute-start(bf16[512,512]{1,0:T(8,128)(2,1)S(1)} %broadcast_select_fusion.8), channel_id=1, source_target_pairs={{0,16},{16,0},{4,20},{20,4},{8,24},{24,8},{12,28},{28,12},{1,17},{... | collective-permute-start | bytes 1572872 | tf_op jit(solution)/shard_map/ppermute | solution.py:21
  46.6 2.0 collective-permute-start.3
  48.6 17.2 %copy-start.1 = (bf16[4,512,512]{2,1,0:T(8,128)(2,1)S(1)}, bf16[4,512,512]{2,1,0:T(8,128)(2,1)}, u32[]{:S(2)}) copy-start(bf16[4,512,512]{2,1,0:T(8,128)(2,1)} %convert_element_type.79) | copy-start | bytes 6291460
  48.6 14.0 %collective-permute-start.4 = (bf16[512,512]{1,0:T(8,128)(2,1)S(1)}, bf16[512,512]{1,0:T(8,128)(2,1)S(1)}, u32[]{:S(2)}, u32[]{:S(2)}) collective-permute-start(bf16[512,512]{1,0:T(8,128)(2,1)S(1)} %broadcast_select_fusion.5), channel_id=1, source_target_pairs={{0,8},{8,0},{4,12},{12,4},{16,24},{24,16},{20,28},{28,20},{1,9},{9... | collective-permute-start | bytes 1572872 | tf_op jit(solution)/shard_map/ppermute | solution.py:21
  62.7 13.2 %collective-permute-start.5 = (bf16[512,512]{1,0:T(8,128)(2,1)S(1)}, bf16[512,512]{1,0:T(8,128)(2,1)S(1)}, u32[]{:S(2)}, u32[]{:S(2)}) collective-permute-start(bf16[512,512]{1,0:T(8,128)(2,1)S(1)} %broadcast_select_fusion.7), channel_id=1, source_target_pairs={{0,16},{16,0},{4,20},{20,4},{8,24},{24,8},{12,28},{28,12},{1,17},{... | collective-permute-start | bytes 1572872 | tf_op jit(solution)/shard_map/ppermute | solution.py:21
  76.0 5.0 %copy-start.6 = (f32[1,512]{1,0:T(1,128)S(1)}, f32[1,512]{1,0:T(1,128)}, u32[]{:S(2)}) copy-start(f32[1,512]{1,0:T(1,128)} %param.8) | copy-start | bytes 6148
  81.3 20.7 %copy-start.2 = (bf16[4,512,512]{2,1,0:T(8,128)(2,1)S(1)}, bf16[4,512,512]{2,1,0:T(8,128)(2,1)}, u32[]{:S(2)}) copy-start(bf16[4,512,512]{2,1,0:T(8,128)(2,1)} %convert_element_type.79) | copy-start | bytes 6291460
  81.3 2.0 collective-permute-start.6
  83.3 14.0 %collective-permute-start.7 = (bf16[512,512]{1,0:T(8,128)(2,1)S(1)}, bf16[512,512]{1,0:T(8,128)(2,1)S(1)}, u32[]{:S(2)}, u32[]{:S(2)}) collective-permute-start(bf16[512,512]{1,0:T(8,128)(2,1)S(1)} %broadcast_select_fusion.1), channel_id=1, source_target_pairs={{0,8},{8,0},{4,12},{12,4},{16,24},{24,16},{20,28},{28,20},{1,9},{9... | collective-permute-start | bytes 1572872 | tf_op jit(solution)/shard_map/ppermute | solution.py:21
  98.2 13.4 %collective-permute-start.8 = (bf16[512,512]{1,0:T(8,128)(2,1)}, bf16[512,512]{1,0:T(8,128)(2,1)}, u32[]{:S(2)}, u32[]{:S(2)}) collective-permute-start(bf16[512,512]{1,0:T(8,128)(2,1)} %broadcast_select_fusion.3), channel_id=1, source_target_pairs={{0,16},{16,0},{4,20},{20,4},{8,24},{24,8},{12,28},{28,12},{1,17},{... | collective-permute-start | bytes 1572872 | tf_op jit(solution)/shard_map/ppermute | solution.py:21
  111.7 2.5 copy-start.5
  111.7 2.5 copy-start.10
  114.1 4.2 %collective-permute-start.9 = (bf16[512,512]{1,0:T(8,128)(2,1)S(1)}, bf16[512,512]{1,0:T(8,128)(2,1)S(1)}, u32[]{:S(2)}, u32[]{:S(2)}) collective-permute-start(bf16[512,512]{1,0:T(8,128)(2,1)S(1)} %convolution_convert_fusion.1), channel_id=1, source_target_pairs={{0,4},{4,0},{8,12},{12,8},{16,20},{20,16},{24,28},{28,24},{1,5},{5... | collective-permute-start | bytes 1572872 | tf_op jit(solution)/shard_map/ppermute | solution.py:21
  115.8 4.8 %copy-start.3 = (bf16[512,512]{1,0:T(8,128)(2,1)S(1)}, bf16[512,512]{1,0:T(8,128)(2,1)}, u32[]{:S(2)}) copy-start(bf16[512,512]{1,0:T(8,128)(2,1)} %gather_fusion.1) | copy-start | bytes 1572868
  119.2 16.5 %collective-permute-start.10 = (bf16[512,512]{1,0:T(8,128)(2,1)}, bf16[512,512]{1,0:T(8,128)(2,1)}, u32[]{:S(2)}, u32[]{:S(2)}) collective-permute-start(bf16[512,512]{1,0:T(8,128)(2,1)} %broadcast_select_fusion), channel_id=1, source_target_pairs={{0,8},{8,0},{4,12},{12,4},{16,24},{24,16},{20,28},{28,20},{1,9},{9... | collective-permute-start | bytes 1572872 | tf_op jit(solution)/shard_map/ppermute | solution.py:21
  137.6 55.6 %collective-permute-start.11 = (bf16[512,512]{1,0:T(8,128)(2,1)}, bf16[512,512]{1,0:T(8,128)(2,1)}, u32[]{:S(2)}, u32[]{:S(2)}) collective-permute-start(bf16[512,512]{1,0:T(8,128)(2,1)} %broadcast_select_fusion.2), channel_id=1, source_target_pairs={{0,16},{16,0},{4,20},{20,4},{8,24},{24,8},{12,28},{28,12},{1,17},{... | collective-permute-start | bytes 1572872 | tf_op jit(solution)/shard_map/ppermute | solution.py:21
Sparse Core Ops, SparseCore 0:
  124.5 144.1 all-reduce.1
where the time goes:
time: 283 us; the launch traced here: 282 us
  waiting for transfers between devices  141 us (50%)
  blocking collectives  47.6 us (17%)
  other arithmetic  24 us (8%)
  matrix products  23.4 us (8%)
  between operations  21.5 us (8%)
  starting transfers between devices  14.2 us (5%)
  local copies, waits for them, and re-layouts  10.4 us (4%)
    ppermute x12, waiting for transfers between devices, from_partner(): return lax.ppermute(block, axis, route)  73.1 us
    psum x1, waiting for transfers between devices, body(): rel_total, loss_total = lax.psum((rel_sum, loss_sum), ('dom', 'grp'))  67.8 us
    psum x1, blocking collectives, body(): rel_total, loss_total = lax.psum((rel_sum, loss_sum), ('dom', 'grp'))  47.6 us
    ppermute x12, starting transfers between devices, from_partner(): return lax.ppermute(block, axis, route)  14.2 us
    scatter-add x2, other arithmetic, apply_back(): jnp.zeros((row_count, src_grad.shape[1]), jnp.float32).at[src_idx]  9.51 us
    dot_general x2, matrix products, apply_back(): jnp.einsum('ef,kdf->ked', dquery, rel_b, preferred_element_type=jnp.float32)  5.7 us
  transfers between devices with their start and end apart: 13, of which 10 were waited for; matrix products, arithmetic and copies ran while one was open for 14% of the time, Pallas kernels for 0%

commit v1 on v0

v1 whole, which is shorter than its diff:
```python
import jax
import jax.numpy as jnp
from jax import lax
from jax.sharding import PartitionSpec as P

EDGES = 512
ROUNDS = 2


LEARN_RATE = 0.1
EPSILON = 1e-08
DIGIT = 3
RADIX = 128


def xor_route(axis, mask):
    return [(low, low ^ mask) for low in range(lax.axis_size(axis))]


def exchange(block, axis, mask):
    bits = lax.axis_size(axis).bit_length() - 1
    done = 0
    while done < bits:
        width = min(DIGIT, bits - done)
        digit = jnp.bitwise_and(jnp.right_shift(mask, done), (1 << width) - 1)
        branches = [lambda x: x]
        for value in range(1, 1 << width):
            route = xor_route(axis, value << done)
            branches.append(lambda x, route=route: lax.ppermute(x, axis, route))
        block = lax.switch(digit, branches, block)
        done += width
    return block


def project(src_b, rel_idx, rel_b):
    projected = jnp.einsum("ed,kdf->kef", src_b, rel_b, preferred_element_type=jnp.float32)
    onehot = (rel_idx[None, :] == jnp.arange(rel_b.shape[0], dtype=jnp.int32)[:, None]).astype(
        jnp.float32
    )
    return jnp.sum(onehot[:, :, None] * projected, axis=0).astype(jnp.bfloat16), onehot


def score(queries, block_b, dst_idx):
    scores = jnp.dot(queries, block_b.T, preferred_element_type=jnp.float32)
    row_max = jnp.max(scores, axis=1, keepdims=True)
    exp_scores = jnp.exp(scores - row_max)
    row_total = jnp.sum(exp_scores, axis=1, keepdims=True)
    targets = (dst_idx[:, None] == jnp.arange(block_b.shape[0], dtype=jnp.int32)[None, :]).astype(
        jnp.float32
    )
    edge_loss = row_max[:, 0] + jnp.log(row_total[:, 0]) - jnp.sum(scores * targets, axis=1)
    deltas = (exp_scores / row_total - targets).astype(jnp.bfloat16)
    return jnp.sum(edge_loss), deltas


def encode(idx, width):
    rows = []
    for part in idx:
        rows += [part // RADIX, part % RADIX]
    rows = jnp.stack(rows).astype(jnp.bfloat16)
    return jnp.pad(rows, ((0, 16 - rows.shape[0]), (0, 0)))


def decode(rows):
    rows = rows.astype(jnp.float32).astype(jnp.int32)
    return [rows[2 * n] * RADIX + rows[2 * n + 1] for n in range(3)]


def pieces(total):
    high = total.astype(jnp.bfloat16)
    rest = total - high.astype(jnp.float32)
    mid = rest.astype(jnp.bfloat16)
    low = (rest - mid.astype(jnp.float32)).astype(jnp.bfloat16)
    return [high, mid, low]


def all_sum(value, loss):
    dom, grp = lax.axis_size("dom"), lax.axis_size("grp")
    me_d, me_g = lax.axis_index("dom"), lax.axis_index("grp")
    bits_d, bits_g = dom.bit_length() - 1, grp.bit_length() - 1
    up = list(range(1, bits_d))
    stages = []
    if bits_d:
        stages.append(("dom", 0, 0))
    stages += [("dom", a, b) for a, b in zip(up, up[::-1])]
    stages += [("grp", bit, bit) for bit in range(bits_g)]
    odd = jnp.bitwise_and(me_d, 1)

    def send(block, axis, even_bit, odd_bit):
        count = lax.axis_size(axis)
        if even_bit == odd_bit:
            route = [(n, n ^ (1 << even_bit)) for n in range(count)]
        else:
            route = [(n, n ^ (1 << (odd_bit if n & 1 else even_bit))) for n in range(count)]
        return lax.ppermute(block, axis, route)

    def bit_of(axis, even_bit, odd_bit):
        me = me_d if axis == "dom" else me_g
        bit = jnp.where(odd == 1, odd_bit, even_bit)
        return jnp.bitwise_and(jnp.right_shift(me, bit), 1) == 1

    cols = value.shape[1]
    for axis, a, b in stages:
        half = value.shape[0] // 2
        upper = bit_of(axis, a, b)
        low, high = value[:half], value[half:]
        keep = jnp.where(upper, high, low)
        give = jnp.where(upper, low, high).astype(jnp.bfloat16)
        tail = jnp.stack([jnp.broadcast_to(p, (cols,)) for p in pieces(loss)])
        tail = jnp.pad(tail, ((0, 13), (0, 0)))
        came = send(jnp.concatenate([give, tail]), axis, a, b).astype(jnp.float32)
        value = keep + came[:half]
        loss = loss + (came[half, 0] + came[half + 1, 0] + came[half + 2, 0])
    value = value.astype(jnp.bfloat16)
    for axis, a, b in stages[::-1]:
        upper = bit_of(axis, a, b)
        came = send(value, axis, a, b)
        value = jnp.concatenate(
            [jnp.where(upper, came, value), jnp.where(upper, value, came)]
        )
    return value.astype(jnp.float32), loss


def body(embeddings, ada_state, relations, plan, src_rows, dst_rows, rel_ids):
    own_rows = embeddings[0]
    row_state = ada_state[0]
    rel_b = relations.astype(jnp.bfloat16)
    row_count, width = own_rows.shape
    loss_sum = jnp.zeros((), jnp.float32)
    rel_sum = jnp.zeros(relations.shape, jnp.float32)
    for round_no in range(ROUNDS):
        src_idx = src_rows[0, 0, round_no]
        dst_idx = dst_rows[0, 0, round_no]
        rel_idx = rel_ids[0, 0, round_no]
        own_b = own_rows.astype(jnp.bfloat16)
        payload = jnp.concatenate([own_b, encode((src_idx, dst_idx, rel_idx), width)])
        payload = exchange(payload, "dom", plan[round_no])
        src_b = own_b[src_idx]
        queries, onehot = project(src_b, rel_idx, rel_b)
        pair_b = payload[:row_count]
        pair_src, pair_dst, pair_rel = decode(payload[row_count:])
        edge_loss, deltas = score(queries, pair_b, dst_idx)
        dquery = jnp.dot(deltas, pair_b, preferred_element_type=jnp.float32).astype(jnp.bfloat16)
        pair_queries, _ = project(pair_b[pair_src], pair_rel, rel_b)
        _, pair_deltas = score(pair_queries, own_b, pair_dst)
        dblock = lax.dot_general(
            pair_deltas,
            pair_queries,
            (((0,), (0,)), ((), ())),
            preferred_element_type=jnp.float32,
        ).astype(jnp.bfloat16)
        back = jnp.einsum("ef,kdf->ked", dquery, rel_b, preferred_element_type=jnp.float32)
        src_grad = jnp.sum(onehot[:, :, None] * back, axis=0)
        gradient = jnp.zeros((row_count, width), jnp.float32).at[src_idx].add(src_grad)
        masked = (onehot[:, :, None] * dquery.astype(jnp.float32)).astype(jnp.bfloat16)
        rel_part = jnp.einsum("ed,kef->kdf", src_b, masked, preferred_element_type=jnp.float32)
        gradient = gradient + dblock.astype(jnp.float32)
        row_state = row_state + jnp.mean(gradient * gradient, axis=-1)
        own_rows = own_rows - LEARN_RATE * gradient / (jnp.sqrt(row_state)[:, None] + EPSILON)
        loss_sum = loss_sum + edge_loss
        rel_sum = rel_sum + rel_part
    rel_total, loss_total = all_sum(rel_sum.reshape(-1, width), loss_sum)
    mean_loss = loss_total / (lax.axis_size("dom") * lax.axis_size("grp") * ROUNDS * EDGES)
    return (own_rows[None], row_state[None], rel_total.reshape(relations.shape), mean_loss)


def solution(mesh):
    return jax.shard_map(
        body,
        mesh=mesh,
        in_specs=(
            P("grp", "dom", None),
            P("grp", "dom"),
            P(),
            P(),
            P("grp", "dom", None, None),
            P("grp", "dom", None, None),
            P("grp", "dom", None, None),
        ),
        out_specs=(P("grp", "dom", None), P("grp", "dom"), P(), P()),
        check_vma=False,
    )
```

time: 283 us -> 180 us (0.64)
  waiting for transfers between devices: 141 us -> 50.3 us
  blocking collectives: 47.6 us -> 0 us
  other arithmetic: 24 us -> 41.5 us
  starting transfers between devices: 14.2 us -> 25.4 us
  local copies, waits for them, and re-layouts: 10.4 us -> 19.9 us
  between operations: 21.5 us -> 14.8 us
  matrix products: 23.4 us -> 27.4 us
    psum x1 -> x0, waiting for transfers between devices: 67.8 us -> none  [body(): rel_total, loss_total = lax.psum((rel_sum, loss_sum), ('dom', 'grp'))]
    psum x1 -> x0, blocking collectives: 47.6 us -> none  [body(): rel_total, loss_total = lax.psum((rel_sum, loss_sum), ('dom', 'grp'))]
    ppermute x12, waiting for transfers between devices: 73.1 us -> 50.3 us  [the longest x10 25.3 us: send(): return lax.ppermute(block, axis, route)]
    ppermute x12, starting transfers between devices: 14.2 us -> 25.4 us  [the longest x10 19.8 us: send(): return lax.ppermute(block, axis, route)]
    another operation x0 -> x12, other arithmetic: none -> 4.2 us
    concatenate x0 -> x17, other arithmetic: none -> 4.18 us  [the longest x10 2.86 us: all_sum(): came = send(jnp.concatenate([give, tail]), axis, a, b).astype(jnp.float32)]
    gather x2 -> x4, local copies, waits for them, and re-layouts: 3.8 us -> 7.87 us  [the longest x2 3.94 us: body(): src_b = own_b[src_idx]]
    dot_general x12 -> x16, matrix products: 23.4 us -> 27.4 us  [the longest x4 10.8 us: project(): jnp.einsum('ed,kdf->kef', src_b, rel_b, preferred_element_type=jnp.float32)]
  transfers between devices with their start and end apart: 13 -> 12, of which waited for: 10 -> 8; matrix products, arithmetic and copies ran while one was open for 14% -> 11% of each run, Pallas kernels for 0% -> 0%
where the time goes in v1:
time: 180 us; the launch traced here: 179 us
  waiting for transfers between devices  50.3 us (28%)
  other arithmetic  41.5 us (23%)
  matrix products  27.4 us (15%)
  starting transfers between devices  25.4 us (14%)
  local copies, waits for them, and re-layouts  19.9 us (11%)
  between operations  14.8 us (8%)
    ppermute x10, waiting for transfers between devices, send(): return lax.ppermute(block, axis, route)  25.3 us
    ppermute x2, waiting for transfers between devices, exchange(): branches.append(lambda x, route=route: lax.ppermute(x, axis, route))  25 us
    ppermute x10, starting transfers between devices, send(): return lax.ppermute(block, axis, route)  19.8 us
    dot_general x4, matrix products, project(): jnp.einsum('ed,kdf->kef', src_b, rel_b, preferred_element_type=jnp.float32)  10.8 us
    scatter-add x2, other arithmetic, body(): jnp.zeros((row_count, width), jnp.float32).at[src_idx].add(src_grad)  9.58 us
    unnamed x30, local copies, waits for them, and re-layouts  6.26 us
    ppermute x2, starting transfers between devices, exchange(): branches.append(lambda x, route=route: lax.ppermute(x, axis, route))  5.6 us
    dot_general x2, matrix products, body(): jnp.einsum('ed,kef->kdf', src_b, masked, preferred_element_type=jnp.float32)  4.97 us
  transfers between devices with their start and end apart: 12, of which 8 were waited for; matrix products, arithmetic and copies ran while one was open for 11% of the time, Pallas kernels for 0%

profile of v1, /device:TPU:0, one launch (start us, length us, event | category | flops | bytes accessed | tf_op | source)
XLA Modules:
  0.0 179.4 jit_solution(15182926689826574175)
XLA Ops:
  0.6 0.8 fusion.84
  1.4 0.7 fusion.59
  2.1 0.8 fusion.85
  2.9 0.7 fusion.60
  3.6 1.3 fusion.86
  5.5 0.8 compare_select_fusion
  6.3 0.8 fusion.63
  7.1 0.8 fusion.58
  7.9 1.3 bitcast_convert_fusion
  9.2 0.8 fusion.67
  10.1 15.2 %conditional.2 = (bf16[528,512]{1,0:T(8,128)(2,1)S(1)}) conditional(s32[]{:T(128)} %bitcast.1, bf16[528,512]{1,0:T(8,128)(2,1)S(1)} %fusion.19, bf16[528,512]{1,0:T(8,128)(2,1)S(1)} %fusion.19, bf16[528,512]{1,0:T(8,128)(2,1)S(1)} %fusion.19, bf16[528,512]{1,0:T(8,128)(2,1)S(1)} %fusion.19, ...), branch_computations={%region_0.1_spmd, %region_1.2_spmd, %region_2.3_spmd, %region_3.4_... | conditional | bytes 3244080 | solution.py:30
  10.2 2.5 %collective-permute-start.2 = (bf16[528,512]{1,0:T(8,128)(2,1)S(1)}, bf16[528,512]{1,0:T(8,128)(2,1)S(1)}, u32[]{:S(2)}, u32[]{:S(2)}) collective-permute-start(bf16[528,512]{1,0:T(8,128)(2,1)S(1)} %param.3), channel_id=1, source_target_pairs={{0,12},{4,8},{8,4},{12,0},{16,28},{20,24},{24,20},{28,16},{1,13},{... | collective-permute-start | bytes 1622024 | tf_op jit(solution)/shard_map/cond/branch_3_fun/ppermute | solution.py:29
  12.6 12.7 %collective-permute-done.2 = bf16[528,512]{1,0:T(8,128)(2,1)S(1)} collective-permute-done((bf16[528,512]{1,0:T(8,128)(2,1)S(1)}, bf16[528,512]{1,0:T(8,128)(2,1)S(1)}, u32[]{:S(2)}, u32[]{:S(2)}) %collective-permute-start.2) | collective-permute-done | bytes 540704 | tf_op jit(solution)/shard_map/cond/branch_3_fun/ppermute | solution.py:29
  26.2 2.0 %gather_fusion.1 = bf16[512,512]{1,0:T(8,128)(2,1)S(1)} fusion(bf16[512,512]{1,0:T(8,128)(2,1)S(1)} %bitcast_convert_fusion, s32[1024]{0:T(1024)S(1)} %pad_clamp_fusion.2), kind=kCustom, calls=%fused_computation.1 | custom fusion | bytes 1050624 | tf_op jit(solution)/shard_map/gather | solution.py:138
  28.2 2.5 %convert_element_type.248 = bf16[4,512,512]{2,1,0:T(8,128)(2,1)S(1)} convert(f32[4,512,512]{2,1,0:T(8,128)} %param.25) | non-fusion elementwise | flops 1048576 | bytes 6291456 | tf_op jit(solution)/shard_map/convert_element_type | solution.py:127
  30.7 1.3 fusion.4
  32.8 1.5 fusion.91
  34.3 0.6 subtract_reduce_fusion.1
  34.9 2.0 %gather_fusion = bf16[512,512]{1,0:T(8,128)(2,1)S(1)} fusion(bf16[512,512]{1,0:T(8,128)(2,1)S(1)} %slice.229, s32[1024]{0:T(1024)S(1)} %pad_clamp_fusion.3), kind=kCustom, calls=%fused_computation | custom fusion | bytes 1050624 | tf_op jit(solution)/shard_map/gather | solution.py:144
  36.9 2.9 %fusion.5 = bf16[512,512]{1,0:T(8,128)(2,1)S(1)} fusion(bf16[4,512,512]{2,1,0:T(8,128)(2,1)} %copy-done.7, f32[4,512]{1,0:T(4,128)S(1)} %fusion.52, bf16[512,512]{1,0:T(8,128)(2,1)S(1)} %gather_fusion), kind=kOutput, calls=%fused_computation.17 | convolution fusion | flops 1075576832 | bytes 3153920 | tf_op jit(solution)/shard_map/ed,kdf->kef/dot_general | solution.py:36
  40.2 1.1 copy-done.8
  41.3 2.3 %fusion.3 = f32[512,512]{1,0:T(8,128)} fusion(bf16[4,512,512]{2,1,0:T(8,128)(2,1)S(1)} %copy-done.8, f32[4,512]{1,0:T(4,128)S(1)} %fusion.53, bf16[512,512]{1,0:T(8,128)(2,1)S(1)} %get-tuple-element.109), kind=kOutput, calls=%fused_computation.13 | convolution fusion | flops 1075576832 | bytes 3678208 | tf_op jit(solution)/shard_map/ef,kdf->ked/dot_general | solution.py:152
  44.3 4.9 %scatter_fusion = f32[512,512]{1,0:T(8,128)S(1)} fusion(f32[512,512]{1,0:T(8,128)S(1)} %fusion.11, s32[512]{0:T(512)S(1)} %bitcast.216, f32[512,512]{1,0:T(8,128)} %fusion.3), kind=kCustom, calls=%fused_computation.4 | custom fusion | flops 262144 | bytes 3147776 | tf_op jit(solution)/shard_map/scatter-add | solution.py:154
  49.7 2.0 %gather_fusion.3 = bf16[512,512]{1,0:T(8,128)(2,1)S(1)} fusion(bf16[512,512]{1,0:T(8,128)(2,1)S(1)} %fusion.78, s32[1024]{0:T(1024)S(1)} %pad_clamp_fusion), kind=kCustom, calls=%fused_computation.3 | custom fusion | bytes 1050624 | tf_op jit(solution)/shard_map/gather | solution.py:138
  51.7 3.8 %fusion.1 = bf16[512,512]{1,0:T(8,128)(2,1)} fusion(bf16[4,512,512]{2,1,0:T(8,128)(2,1)} %copy-done.7, f32[4,512]{1,0:T(4,128)S(1)} %fusion.55, bf16[512,512]{1,0:T(8,128)(2,1)S(1)} %gather_fusion.3), kind=kOutput, calls=%fused_computation.9 | convolution fusion | flops 1075576832 | bytes 3153920 | tf_op jit(solution)/shard_map/ed,kdf->kef/dot_general | solution.py:36
  55.5 15.5 %conditional.3 = (bf16[528,512]{1,0:T(8,128)(2,1)S(1)}) conditional(s32[]{:T(128)} %bitcast.20, bf16[528,512]{1,0:T(8,128)(2,1)S(1)} %fusion.20, bf16[528,512]{1,0:T(8,128)(2,1)S(1)} %fusion.20, bf16[528,512]{1,0:T(8,128)(2,1)S(1)} %fusion.20, bf16[528,512]{1,0:T(8,128)(2,1)S(1)} %fusion.20, ...), branch_computations={%region_17.18_spmd, %region_18.19_spmd, %region_19.20_spmd, %regio... | conditional | bytes 3244080 | solution.py:30
  55.5 3.1 %collective-permute-start.13 = (bf16[528,512]{1,0:T(8,128)(2,1)S(1)}, bf16[528,512]{1,0:T(8,128)(2,1)S(1)}, u32[]{:S(2)}, u32[]{:S(2)}) collective-permute-start(bf16[528,512]{1,0:T(8,128)(2,1)S(1)} %param.15), channel_id=1, source_target_pairs={{0,28},{4,24},{8,20},{12,16},{16,12},{20,8},{24,4},{28,0},{1,29},{... | collective-permute-start | bytes 1622024 | tf_op jit(solution)/shard_map/cond/branch_7_fun/ppermute | solution.py:29
  58.6 12.4 %collective-permute-done.13 = bf16[528,512]{1,0:T(8,128)(2,1)S(1)} collective-permute-done((bf16[528,512]{1,0:T(8,128)(2,1)S(1)}, bf16[528,512]{1,0:T(8,128)(2,1)S(1)}, u32[]{:S(2)}, u32[]{:S(2)}) %collective-permute-start.13) | collective-permute-done | bytes 540704 | tf_op jit(solution)/shard_map/cond/branch_7_fun/ppermute | solution.py:29
  71.0 1.5 fusion.90
  72.9 1.7 fusion.92
  74.5 0.6 subtract_reduce_fusion
  76.5 3.0 %fusion.6 = f32[4,512,512]{1,2,0:T(8,128)S(1)} fusion(f32[512,512]{1,0:T(8,128)} %get-tuple-element.108, f32[4,512]{1,0:T(4,128)S(1)} %fusion.53, bf16[512,512]{1,0:T(8,128)(2,1)S(1)} %gather_fusion.1), kind=kOutput, calls=%fused_computation.21 | convolution fusion | flops 1075838976 | bytes 5775360 | tf_op jit(solution)/shard_map/ed,kef->kdf/dot_general | solution.py:156
  79.5 2.0 %add_bitcast_fusion = f32[4,512,512]{2,1,0:T(8,128)S(1)} fusion(f32[4,512,512]{1,2,0:T(8,128)S(1)} %fusion.6, f32[512,512]{1,0:T(8,128)S(1)} %copy-done.10, f32[4,512]{1,0:T(4,128)S(1)} %fusion.55, bf16[512,512]{1,0:T(8,128)(2,1)S(1)} %gather_fusion.3), kind=kOutput, calls=%fused_computation.18 | convolution fusion | flops 1076887552 | bytes 9969664 | tf_op jit(solution)/shard_map/ed,kef->kdf/dot_general | solution.py:156
  81.7 1.6 pad_maximum_fusion.1
  84.2 4.0 %slice_select_fusion = f32[2,512,512]{2,1,0:T(8,128)} fusion(f32[4,512,512]{2,1,0:T(8,128)} %copy-done, pred[]{:T(512)S(6)} %eq.201), kind=kLoop, calls=%fused_computation.29 | loop fusion | flops 524288 | bytes 6291457 | tf_op jit(solution)/shard_map/jit(_where)/select_n | solution.py:107
  91.1 1.2 copy-done.4
  92.8 1.3 copy-done.1
  94.4 2.0 %collective-permute-start.15 = (bf16[528,512]{1,0:T(8,128)(2,1)S(1)}, bf16[528,512]{1,0:T(8,128)(2,1)S(1)}, u32[]{:S(2)}, u32[]{:S(2)}) collective-permute-start(bf16[528,512]{1,0:T(8,128)(2,1)S(1)} %pad_maximum_fusion.3), channel_id=1, source_target_pairs={{0,8},{4,20},{8,0},{12,28},{16,24},{20,4},{24,16},{28,12},{1,9},{5... | collective-permute-start | bytes 1622024 | tf_op jit(solution)/shard_map/ppermute | solution.py:95
  96.4 7.4 %collective-permute-done.15 = bf16[528,512]{1,0:T(8,128)(2,1)S(1)} collective-permute-done((bf16[528,512]{1,0:T(8,128)(2,1)S(1)}, bf16[528,512]{1,0:T(8,128)(2,1)S(1)}, u32[]{:S(2)}, u32[]{:S(2)}) %collective-permute-start.15) | collective-permute-done | bytes 540704 | tf_op jit(solution)/shard_map/ppermute | solution.py:95
  106.5 1.9 %slice_add_fusion.1 = f32[512,512]{1,0:T(8,128)S(1)} fusion(f32[528,512]{1,0:T(8,128)S(1)} %convert_element_type.291, f32[1024,512]{1,0:T(8,128)} %copy-done.1, pred[]{:T(512)S(6)} %eq.203), kind=kLoop, calls=%fused_computation.40 | loop fusion | flops 524288 | bytes 4194305 | tf_op jit(solution)/shard_map/add | solution.py:112
  108.5 0.8 pad_maximum_fusion.5
  109.3 1.9 %collective-permute-start.16 = (bf16[272,512]{1,0:T(8,128)(2,1)}, bf16[272,512]{1,0:T(8,128)(2,1)S(1)}, u32[]{:S(2)}, u32[]{:S(2)}) collective-permute-start(bf16[272,512]{1,0:T(8,128)(2,1)} %pad_maximum_fusion.5), channel_id=1, source_target_pairs={{0,16},{4,12},{8,24},{12,4},{16,0},{20,28},{24,8},{28,20},{1,17},{... | collective-permute-start | bytes 835592 | tf_op jit(solution)/shard_map/ppermute | solution.py:95
  111.3 4.8 %collective-permute-done.16 = bf16[272,512]{1,0:T(8,128)(2,1)S(1)} collective-permute-done((bf16[272,512]{1,0:T(8,128)(2,1)}, bf16[272,512]{1,0:T(8,128)(2,1)S(1)}, u32[]{:S(2)}, u32[]{:S(2)}) %collective-permute-start.16) | collective-permute-done | bytes 278560 | tf_op jit(solution)/shard_map/ppermute | solution.py:95
  118.9 0.8 copy-done.5
  119.8 2.1 %collective-permute-start.17 = (bf16[144,512]{1,0:T(8,128)(2,1)S(1)}, bf16[144,512]{1,0:T(8,128)(2,1)S(1)}, u32[]{:S(2)}, u32[]{:S(2)}) collective-permute-start(bf16[144,512]{1,0:T(8,128)(2,1)S(1)} %pad_maximum_fusion.7), channel_id=1, source_target_pairs={{0,1},{1,0},{2,3},{3,2},{4,5},{5,4},{6,7},{7,6},{8,9},{9,8},{10,11... | collective-permute-start | bytes 442376 | tf_op jit(solution)/shard_map/ppermute | solution.py:95
  121.8 3.1 %collective-permute-done.17 = bf16[144,512]{1,0:T(8,128)(2,1)S(1)} collective-permute-done((bf16[144,512]{1,0:T(8,128)(2,1)S(1)}, bf16[144,512]{1,0:T(8,128)(2,1)S(1)}, u32[]{:S(2)}, u32[]{:S(2)}) %collective-permute-start.17) | collective-permute-done | bytes 147488 | tf_op jit(solution)/shard_map/ppermute | solution.py:95
  127.7 1.1 slice_add_fusion.3
  128.9 3.1 %collective-permute-start.18 = (bf16[80,512]{1,0:T(8,128)(2,1)S(1)}, bf16[80,512]{1,0:T(8,128)(2,1)S(1)}, u32[]{:S(2)}, u32[]{:S(2)}) collective-permute-start(bf16[80,512]{1,0:T(8,128)(2,1)S(1)} %pad_maximum_fusion.9), channel_id=1, source_target_pairs={{0,2},{1,3},{2,0},{3,1},{4,6},{5,7},{6,4},{7,5},{8,10},{9,11},{10,... | collective-permute-start | bytes 245768 | tf_op jit(solution)/shard_map/ppermute | solution.py:95
  132.0 2.4 %collective-permute-done.18 = bf16[80,512]{1,0:T(8,128)(2,1)S(1)} collective-permute-done((bf16[80,512]{1,0:T(8,128)(2,1)S(1)}, bf16[80,512]{1,0:T(8,128)(2,1)S(1)}, u32[]{:S(2)}, u32[]{:S(2)}) %collective-permute-start.18) | collective-permute-done | bytes 81952 | tf_op jit(solution)/shard_map/ppermute | solution.py:95
  134.4 3.1 %collective-permute-start.19 = (bf16[64,512]{1,0:T(8,128)(2,1)S(1)}, bf16[64,512]{1,0:T(8,128)(2,1)S(1)}, u32[]{:S(2)}, u32[]{:S(2)}) collective-permute-start(bf16[64,512]{1,0:T(8,128)(2,1)S(1)} %fusion.51), channel_id=1, source_target_pairs={{0,2},{1,3},{2,0},{3,1},{4,6},{5,7},{6,4},{7,5},{8,10},{9,11},{10,... | collective-permute-start | bytes 196616 | tf_op jit(solution)/shard_map/ppermute | solution.py:95
  137.5 2.0 %gather_fusion.2 = bf16[512,512]{1,0:T(8,128)(2,1)S(1)} fusion(bf16[512,512]{1,0:T(8,128)(2,1)S(1)} %slice.237, s32[1024]{0:T(1024)S(1)} %pad_clamp_fusion.1), kind=kCustom, calls=%fused_computation.2 | custom fusion | bytes 1050624 | tf_op jit(solution)/shard_map/gather | solution.py:144
  140.0 4.2 %collective-permute-start.20 = (bf16[128,512]{1,0:T(8,128)(2,1)S(1)}, bf16[128,512]{1,0:T(8,128)(2,1)S(1)}, u32[]{:S(2)}, u32[]{:S(2)}) collective-permute-start(bf16[128,512]{1,0:T(8,128)(2,1)S(1)} %pad_maximum_fusion.8), channel_id=1, source_target_pairs={{0,1},{1,0},{2,3},{3,2},{4,5},{5,4},{6,7},{7,6},{8,9},{9,8},{10,11... | collective-permute-start | bytes 393224 | tf_op jit(solution)/shard_map/ppermute | solution.py:95
  144.2 2.9 %fusion.2 = bf16[512,512]{1,0:T(8,128)(2,1)S(1)} fusion(bf16[4,512,512]{2,1,0:T(8,128)(2,1)} %copy-done.7, f32[4,512]{1,0:T(4,128)S(1)} %fusion.54, bf16[512,512]{1,0:T(8,128)(2,1)S(1)} %gather_fusion.2), kind=kOutput, calls=%fused_computation.11 | convolution fusion | flops 1075576832 | bytes 3153920 | tf_op jit(solution)/shard_map/ed,kdf->kef/dot_general | solution.py:36
  147.2 1.6 collective-permute-start.21
  149.5 7.0 %collective-permute-done.21 = bf16[256,512]{1,0:T(8,128)(2,1)S(1)} collective-permute-done((bf16[256,512]{1,0:T(8,128)(2,1)S(1)}, bf16[256,512]{1,0:T(8,128)(2,1)S(1)}, u32[]{:S(2)}, u32[]{:S(2)}) %collective-permute-start.21) | collective-permute-done | bytes 262176 | tf_op jit(solution)/shard_map/ppermute | solution.py:95
  156.6 1.6 collective-permute-start.22
  158.7 1.1 copy-done.9
  159.9 2.3 %fusion = f32[512,512]{1,0:T(8,128)} fusion(bf16[4,512,512]{2,1,0:T(8,128)(2,1)S(1)} %copy-done.9, f32[4,512]{1,0:T(4,128)S(1)} %fusion.55, bf16[512,512]{1,0:T(8,128)(2,1)S(1)} %copy-done.14), kind=kOutput, calls=%fused_computation.7 | convolution fusion | flops 1075576832 | bytes 3678208 | tf_op jit(solution)/shard_map/ef,kdf->ked/dot_general | solution.py:152
  162.2 4.6 %scatter_fusion.1 = f32[512,512]{1,0:T(8,128)S(1)} fusion(f32[512,512]{1,0:T(8,128)S(1)} %fusion.12, s32[512]{0:T(512)S(1)} %bitcast.214, f32[512,512]{1,0:T(8,128)} %fusion), kind=kCustom, calls=%fused_computation.5 | custom fusion | flops 262144 | bytes 3147776 | tf_op jit(solution)/shard_map/scatter-add | solution.py:154
  166.9 1.3 broadcast_select_fusion.3
  168.2 1.0 pad_maximum_fusion.2
  170.0 1.4 subtract_bitcast_fusion
  173.9 1.6 broadcast_select_fusion.1
  175.6 2.6 %convert.49 = f32[4,512,512]{2,1,0:T(8,128)} convert(bf16[4,512,512]{2,1,0:T(8,128)(2,1)S(1)} %bitcast.211) | non-fusion elementwise | flops 1048576 | bytes 6291456 | tf_op jit(solution)/shard_map/convert_element_type | solution.py:121
  (109 shorter events, 11.9 us)
Async XLA Ops:
  10.1 16.1 %copy-start.11 = (s32[1,1,2,512]{3,2,1,0:T(2,128)S(1)}, s32[1,1,2,512]{3,2,1,0:T(2,128)}, u32[]{:S(2)}) copy-start(s32[1,1,2,512]{3,2,1,0:T(2,128)} %param.29) | copy-start | bytes 12292
  10.1 16.1 %copy-start.12 = (s32[1,1,2,512]{3,2,1,0:T(2,128)S(1)}, s32[1,1,2,512]{3,2,1,0:T(2,128)}, u32[]{:S(2)}) copy-start(s32[1,1,2,512]{3,2,1,0:T(2,128)} %param.28) | copy-start | bytes 12292
  10.2 15.1 %collective-permute-start.2 = (bf16[528,512]{1,0:T(8,128)(2,1)S(1)}, bf16[528,512]{1,0:T(8,128)(2,1)S(1)}, u32[]{:S(2)}, u32[]{:S(2)}) collective-permute-start(bf16[528,512]{1,0:T(8,128)(2,1)S(1)} %param.3), channel_id=1, source_target_pairs={{0,12},{4,8},{8,4},{12,0},{16,28},{20,24},{24,20},{28,16},{1,13},{... | collective-permute-start | bytes 1622024 | tf_op jit(solution)/shard_map/cond/branch_3_fun/ppermute | solution.py:29
  30.7 1.3 copy-start.7
  39.8 1.6 copy-start.8
  44.3 5.1 %copy-start.13 = (f32[1,512]{1,0:T(1,128)S(1)}, f32[1,512]{1,0:T(1,128)}, u32[]{:S(2)}) copy-start(f32[1,512]{1,0:T(1,128)} %param.24) | copy-start | bytes 6148
  44.3 5.1 %copy-start.2 = (f32[1,512,512]{2,1,0:T(8,128)S(1)}, f32[1,512,512]{2,1,0:T(8,128)}, u32[]{:S(2)}) copy-start(f32[1,512,512]{2,1,0:T(8,128)} %param.23) | copy-start | bytes 3145732
  55.5 15.5 %collective-permute-start.13 = (bf16[528,512]{1,0:T(8,128)(2,1)S(1)}, bf16[528,512]{1,0:T(8,128)(2,1)S(1)}, u32[]{:S(2)}, u32[]{:S(2)}) collective-permute-start(bf16[528,512]{1,0:T(8,128)(2,1)S(1)} %param.15), channel_id=1, source_target_pairs={{0,28},{4,24},{8,20},{12,16},{16,12},{20,8},{24,4},{28,0},{1,29},{... | collective-permute-start | bytes 1622024 | tf_op jit(solution)/shard_map/cond/branch_7_fun/ppermute | solution.py:29
  76.5 3.0 %copy-start.10 = (f32[512,512]{1,0:T(8,128)S(1)}, f32[512,512]{1,0:T(8,128)}, u32[]{:S(2)}) copy-start(f32[512,512]{1,0:T(8,128)} %get-tuple-element.110) | copy-start | bytes 3145732
  81.5 2.3 %copy-start = (f32[4,512,512]{2,1,0:T(8,128)}, f32[4,512,512]{2,1,0:T(8,128)S(1)}, u32[]{:S(2)}) copy-start(f32[4,512,512]{2,1,0:T(8,128)S(1)} %add_bitcast_fusion) | copy-start | bytes 12582916
  83.9 4.3 %collective-permute-start.14 = (bf16[1040,512]{1,0:T(8,128)(2,1)}, bf16[1040,512]{1,0:T(8,128)(2,1)S(1)}, u32[]{:S(2)}, u32[]{:S(2)}) collective-permute-start(bf16[1040,512]{1,0:T(8,128)(2,1)} %pad_maximum_fusion.1), channel_id=1, source_target_pairs={{0,4},{4,0},{8,12},{12,8},{16,20},{20,16},{24,28},{28,24},{1,5},{5... | collective-permute-start | bytes 3194888 | tf_op jit(solution)/shard_map/ppermute | solution.py:95
  90.7 1.6 copy-start.4
  92.8 1.3 copy-start.1
  94.4 9.4 %collective-permute-start.15 = (bf16[528,512]{1,0:T(8,128)(2,1)S(1)}, bf16[528,512]{1,0:T(8,128)(2,1)S(1)}, u32[]{:S(2)}, u32[]{:S(2)}) collective-permute-start(bf16[528,512]{1,0:T(8,128)(2,1)S(1)} %pad_maximum_fusion.3), channel_id=1, source_target_pairs={{0,8},{4,20},{8,0},{12,28},{16,24},{20,4},{24,16},{28,12},{1,9},{5... | collective-permute-start | bytes 1622024 | tf_op jit(solution)/shard_map/ppermute | solution.py:95
  109.3 6.8 %collective-permute-start.16 = (bf16[272,512]{1,0:T(8,128)(2,1)}, bf16[272,512]{1,0:T(8,128)(2,1)S(1)}, u32[]{:S(2)}, u32[]{:S(2)}) collective-permute-start(bf16[272,512]{1,0:T(8,128)(2,1)} %pad_maximum_fusion.5), channel_id=1, source_target_pairs={{0,16},{4,12},{8,24},{12,4},{16,0},{20,28},{24,8},{28,20},{1,17},{... | collective-permute-start | bytes 835592 | tf_op jit(solution)/shard_map/ppermute | solution.py:95
  118.9 0.8 copy-start.5
  119.8 5.2 %collective-permute-start.17 = (bf16[144,512]{1,0:T(8,128)(2,1)S(1)}, bf16[144,512]{1,0:T(8,128)(2,1)S(1)}, u32[]{:S(2)}, u32[]{:S(2)}) collective-permute-start(bf16[144,512]{1,0:T(8,128)(2,1)S(1)} %pad_maximum_fusion.7), channel_id=1, source_target_pairs={{0,1},{1,0},{2,3},{3,2},{4,5},{5,4},{6,7},{7,6},{8,9},{9,8},{10,11... | collective-permute-start | bytes 442376 | tf_op jit(solution)/shard_map/ppermute | solution.py:95
  128.9 5.5 %collective-permute-start.18 = (bf16[80,512]{1,0:T(8,128)(2,1)S(1)}, bf16[80,512]{1,0:T(8,128)(2,1)S(1)}, u32[]{:S(2)}, u32[]{:S(2)}) collective-permute-start(bf16[80,512]{1,0:T(8,128)(2,1)S(1)} %pad_maximum_fusion.9), channel_id=1, source_target_pairs={{0,2},{1,3},{2,0},{3,1},{4,6},{5,7},{6,4},{7,5},{8,10},{9,11},{10,... | collective-permute-start | bytes 245768 | tf_op jit(solution)/shard_map/ppermute | solution.py:95
  134.4 5.5 %collective-permute-start.19 = (bf16[64,512]{1,0:T(8,128)(2,1)S(1)}, bf16[64,512]{1,0:T(8,128)(2,1)S(1)}, u32[]{:S(2)}, u32[]{:S(2)}) collective-permute-start(bf16[64,512]{1,0:T(8,128)(2,1)S(1)} %fusion.51), channel_id=1, source_target_pairs={{0,2},{1,3},{2,0},{3,1},{4,6},{5,7},{6,4},{7,5},{8,10},{9,11},{10,... | collective-permute-start | bytes 196616 | tf_op jit(solution)/shard_map/ppermute | solution.py:95
  140.0 7.1 %collective-permute-start.20 = (bf16[128,512]{1,0:T(8,128)(2,1)S(1)}, bf16[128,512]{1,0:T(8,128)(2,1)S(1)}, u32[]{:S(2)}, u32[]{:S(2)}) collective-permute-start(bf16[128,512]{1,0:T(8,128)(2,1)S(1)} %pad_maximum_fusion.8), channel_id=1, source_target_pairs={{0,1},{1,0},{2,3},{3,2},{4,5},{5,4},{6,7},{7,6},{8,9},{9,8},{10,11... | collective-permute-start | bytes 393224 | tf_op jit(solution)/shard_map/ppermute | solution.py:95
  147.2 9.2 %collective-permute-start.21 = (bf16[256,512]{1,0:T(8,128)(2,1)S(1)}, bf16[256,512]{1,0:T(8,128)(2,1)S(1)}, u32[]{:S(2)}, u32[]{:S(2)}) collective-permute-start(bf16[256,512]{1,0:T(8,128)(2,1)S(1)} %pad_maximum_fusion.6), channel_id=1, source_target_pairs={{0,16},{4,12},{8,24},{12,4},{16,0},{20,28},{24,8},{28,20},{1,17},{... | collective-permute-start | bytes 786440 | tf_op jit(solution)/shard_map/ppermute | solution.py:95
  156.6 2.1 %copy-start.6 = (bf16[256,512]{1,0:T(8,128)(2,1)}, bf16[256,512]{1,0:T(8,128)(2,1)S(1)}, u32[]{:S(2)}) copy-start(bf16[256,512]{1,0:T(8,128)(2,1)S(1)} %get-tuple-element.65) | copy-start | bytes 786436
  156.6 10.2 %collective-permute-start.22 = (bf16[512,512]{1,0:T(8,128)(2,1)S(1)}, bf16[512,512]{1,0:T(8,128)(2,1)}, u32[]{:S(2)}, u32[]{:S(2)}) collective-permute-start(bf16[512,512]{1,0:T(8,128)(2,1)S(1)} %pad_maximum_fusion.4), channel_id=1, source_target_pairs={{0,8},{4,20},{8,0},{12,28},{16,24},{20,4},{24,16},{28,12},{1,9},{5... | collective-permute-start | bytes 1572872 | tf_op jit(solution)/shard_map/ppermute | solution.py:95
  158.2 1.6 copy-start.9
  158.2 1.7 copy-start.14
  168.2 1.8 %copy-start.3 = (f32[1,512,512]{2,1,0:T(8,128)S(1)}, f32[1,512,512]{2,1,0:T(8,128)}, u32[]{:S(2)}) copy-start(f32[1,512,512]{2,1,0:T(8,128)} %param.23) | copy-start | bytes 3145732
  169.2 4.6 %collective-permute-start.23 = (bf16[1024,512]{1,0:T(8,128)(2,1)}, bf16[1024,512]{1,0:T(8,128)(2,1)}, u32[]{:S(2)}, u32[]{:S(2)}) collective-permute-start(bf16[1024,512]{1,0:T(8,128)(2,1)} %pad_maximum_fusion.2), channel_id=1, source_target_pairs={{0,4},{4,0},{8,12},{12,8},{16,20},{20,16},{24,28},{28,24},{1,5},{5... | collective-permute-start | bytes 3145736 | tf_op jit(solution)/shard_map/ppermute | solution.py:95

commit v2 on v0

v2 whole, which is shorter than its diff:
```python
import functools
import math

import jax
import jax.numpy as jnp
from jax import lax
from jax.experimental import pallas as pl
from jax.experimental.pallas import tpu as pltpu
from jax.sharding import PartitionSpec as P

EDGES = 512
ROUNDS = 2


LEARN_RATE = 0.1
EPSILON = 1e-08
DIGIT = 3
RADIX_BITS = 7
PAD = 16
NT = (((1,), (1,)), ((), ()))
NN = (((1,), (0,)), ((), ()))
BF = jnp.bfloat16
F32 = jnp.float32
ROW_BLOCK = 16


def mm(a, b, dims=NN):
    return lax.dot_general(a, b, dims, preferred_element_type=F32)


def size_of(shape, dtype):
    return math.prod(shape) * jnp.dtype(dtype).itemsize


def call(kernel, outs, args, flops=0, name=None, room=0):
    moved = sum(size_of(a.shape, a.dtype) for a in args) + sum(size_of(*o) for o in outs)
    return pl.pallas_call(
        kernel,
        out_shape=[jax.ShapeDtypeStruct(s, d) for s, d in outs],
        in_specs=[pl.BlockSpec(memory_space=pltpu.VMEM)] * len(args),
        out_specs=[pl.BlockSpec(memory_space=pltpu.VMEM)] * len(outs),
        compiler_params=pltpu.CompilerParams(vmem_limit_bytes=moved + (1 << 20) + room),
        cost_estimate=pl.CostEstimate(flops=flops, bytes_accessed=moved, transcendentals=0),
        name=name,
    )(*args)


def put_rows(shape, rows):
    at = lax.broadcasted_iota(jnp.int32, shape, 0)
    out = jnp.zeros(shape, F32)
    for n, row in enumerate(rows):
        out = jnp.where(at == n, row, out)
    return out


def encoded(refs, round_no, width):
    rows = []
    for ref in refs:
        idx = ref[round_no : round_no + 1, :]
        rows.append(jnp.right_shift(idx, RADIX_BITS).astype(F32))
        rows.append(jnp.bitwise_and(idx, (1 << RADIX_BITS) - 1).astype(F32))
    return put_rows((PAD, width), rows).astype(BF)


def decoded(tail):
    tail = tail.astype(F32)
    scale = float(1 << RADIX_BITS)
    return [tail[2 * n : 2 * n + 1, :] * scale + tail[2 * n + 1 : 2 * n + 2, :] for n in range(3)]


def columns(rows):
    stacked = put_rows((8, rows[0].shape[1]), rows).T
    return [stacked[:, n : n + 1] for n in range(len(rows))]


def hit_cols(col, count):
    at = lax.broadcasted_iota(jnp.int32, (col.shape[0], count), 1).astype(F32)
    return at == col


def hit_rows(row, count):
    at = lax.broadcasted_iota(jnp.int32, (count, row.shape[1]), 0).astype(F32)
    return at == row


def picked(values, rel_col, k):
    return jnp.where(rel_col == k, values, jnp.zeros_like(values))


def project(src_b, rel_col, rel_ref):
    total = None
    for k in range(rel_ref.shape[0]):
        part = mm(picked(src_b, rel_col, k), rel_ref[k])
        total = part if total is None else total + part
    return total.astype(BF)


def own_edges(queries, pair_b, dst_col):
    scores = mm(queries, pair_b, NT)
    row_max = jnp.max(scores, axis=1, keepdims=True)
    exp_scores = jnp.exp(scores - row_max)
    row_total = jnp.sum(exp_scores, axis=1, keepdims=True)
    target = hit_cols(dst_col, pair_b.shape[0])
    aimed = jnp.sum(jnp.where(target, scores, 0.0), axis=1, keepdims=True)
    loss = jnp.sum(row_max + jnp.log(row_total) - aimed, axis=0, keepdims=True)
    deltas = (exp_scores / row_total - target.astype(F32)).astype(BF)
    return loss, mm(deltas, pair_b).astype(BF)


def pair_edges(own_b, pair_b, tail, rel_ref):
    src_row, dst_row, rel_row = decoded(tail)
    src_col, rel_col = columns([src_row, rel_row])
    rows = own_b.shape[0]
    src_b = mm(hit_cols(src_col, rows).astype(BF), pair_b).astype(BF)
    queries = project(src_b, rel_col, rel_ref)
    scores = mm(own_b, queries, NT)
    top = jnp.max(scores, axis=0, keepdims=True)
    exp_scores = jnp.exp(scores - top)
    total = jnp.sum(exp_scores, axis=0, keepdims=True)
    target = hit_rows(dst_row, rows).astype(F32)
    deltas = (exp_scores / total - target).astype(BF)
    return mm(deltas, queries).astype(BF).astype(F32)


def row_gradient(dquery, src_row, rel_col, rel_ref, rows):
    total = None
    for k in range(rel_ref.shape[0]):
        part = mm(picked(dquery, rel_col, k), rel_ref[k], NT)
        total = part if total is None else total + part
    return mm(hit_rows(src_row, rows).astype(BF), total.astype(BF))


def update(emb_ref, state_ref, gradient, new_ref, new_state_ref):
    rows = gradient.shape[0]
    mean = jnp.mean(gradient * gradient, axis=1, keepdims=True)
    (state,) = columns([state_ref[...]])
    state = state + mean
    scale = LEARN_RATE / (jnp.sqrt(state) + EPSILON)
    new_rows = emb_ref[...] - gradient * scale
    new_ref[...] = new_rows
    new_state_ref[...] = jnp.broadcast_to(state, (rows, 128)).T[0:1, :]
    return new_rows


def index_rows(refs, round_no):
    return [ref[round_no : round_no + 1, :].astype(F32) for ref in refs]


def pack_kernel(emb_ref, src_ref, dst_ref, rid_ref, out_ref):
    rows, width = emb_ref.shape
    out_ref[0:rows, :] = emb_ref[...].astype(BF)
    out_ref[rows : rows + PAD, :] = encoded((src_ref, dst_ref, rid_ref), 0, width)


def project_loop(src_b, rel_col, rel_ref):
    def step(k, total):
        return total + mm(picked(src_b, rel_col, k.astype(F32)), rel_ref[k])

    return lax.fori_loop(0, rel_ref.shape[0], step, jnp.zeros(src_b.shape, F32)).astype(BF)


def query_body(rows_b, src_ref, rid_ref, round_no, rel_ref, query_ref, src_t_ref):
    src_row, rel_row = index_rows((src_ref, rid_ref), round_no)
    src_col, rel_col = columns([src_row, rel_row])
    src_b = mm(hit_cols(src_col, rows_b.shape[0]).astype(BF), rows_b).astype(BF)
    query_ref[...] = project_loop(src_b, rel_col, rel_ref)
    src_t_ref[...] = src_b.T


def first_query_kernel(own_ref, rel_in_ref, src_ref, rid_ref, rel_ref, query_ref, src_t_ref):
    rel_ref[...] = rel_in_ref[...].astype(BF)
    rows = own_ref.shape[0] - PAD
    query_body(own_ref[0:rows, :], src_ref, rid_ref, 0, rel_ref, query_ref, src_t_ref)


def relation_part(src_t_ref, dquery, rel_col, k):
    return mm(src_t_ref[...], picked(dquery, rel_col, k))


def next_query_kernel(
    round_no, own_ref, rel_ref, src_ref, rid_ref, old_t_ref, dquery_ref, query_ref, src_t_ref, part_ref
):
    rows = own_ref.shape[0] - PAD
    query_body(own_ref[0:rows, :], src_ref, rid_ref, round_no, rel_ref, query_ref, src_t_ref)
    (rel_col,) = columns(index_rows((rid_ref,), round_no - 1))

    def step(k, carry):
        part_ref[k] = relation_part(old_t_ref, dquery_ref[...], rel_col, k.astype(F32))
        return carry

    lax.fori_loop(0, rel_ref.shape[0], step, 0)


def round_kernel(
    round_no,
    pair_ref,
    own_ref,
    emb_ref,
    state_ref,
    query_ref,
    rel_ref,
    src_ref,
    dst_ref,
    rid_ref,
    new_ref,
    next_ref,
    new_state_ref,
    dquery_ref,
    loss_ref,
):
    rows, width = emb_ref.shape
    pair_b = pair_ref[0:rows, :]
    src_row, dst_row, rel_row = index_rows((src_ref, dst_ref, rid_ref), round_no)
    dst_col, rel_col = columns([dst_row, rel_row])
    loss, dquery = own_edges(query_ref[...], pair_b, dst_col)
    loss_ref[...] = jnp.broadcast_to(loss, loss_ref.shape)
    dquery_ref[...] = dquery
    gradient = pair_edges(own_ref[0:rows, :], pair_b, pair_ref[rows : rows + PAD, :], rel_ref)
    gradient = gradient + row_gradient(dquery, src_row, rel_col, rel_ref, rows)
    new_rows = update(emb_ref, state_ref, gradient, new_ref, new_state_ref)
    next_ref[0:rows, :] = new_rows.astype(BF)
    next_ref[rows : rows + PAD, :] = encoded((src_ref, dst_ref, rid_ref), round_no + 1, width)


def last_own_kernel(
    round_no,
    stage,
    pair_ref,
    query_ref,
    src_t_ref,
    dst_ref,
    rid_ref,
    part_ref,
    old_loss_ref,
    dquery_ref,
    loss_ref,
    *give_refs,
):
    rows = pair_ref.shape[0] - PAD
    dst_col, rel_col = columns(index_rows((dst_ref, rid_ref), round_no))
    loss, dquery = own_edges(query_ref[...], pair_ref[0:rows, :], dst_col)
    dquery_ref[...] = dquery
    total = old_loss_ref[...] + loss
    loss_ref[...] = total
    upper = stage.upper()
    for n, give_ref in enumerate(give_refs):
        k = 2 * n + 1 - upper
        if n == 0:
            give_ref[0:PAD, :] = loss_tail(total)
            base = PAD
        else:
            base = 0
        part = relation_part(src_t_ref, dquery, rel_col, k.astype(F32)) + part_ref[k]
        give_ref[base : base + part.shape[0], :] = part.astype(BF)


def keep_kernel(round_no, stage, src_t_ref, dquery_ref, rid_ref, part_ref, *keep_refs):
    (rel_col,) = columns(index_rows((rid_ref,), round_no))
    upper = stage.upper()
    for n, keep_ref in enumerate(keep_refs):
        k = 2 * n + upper
        keep_ref[...] = (
            relation_part(src_t_ref, dquery_ref[...], rel_col, k.astype(F32)) + part_ref[k]
        )


def last_rows_kernel(
    round_no,
    pair_ref,
    own_ref,
    emb_ref,
    state_ref,
    dquery_ref,
    rel_ref,
    src_ref,
    rid_ref,
    new_ref,
    new_state_ref,
):
    rows = emb_ref.shape[0]
    src_row, rel_row = index_rows((src_ref, rid_ref), round_no)
    (rel_col,) = columns([rel_row])
    gradient = pair_edges(
        own_ref[0:rows, :], pair_ref[0:rows, :], pair_ref[rows : rows + PAD, :], rel_ref
    )
    gradient = gradient + row_gradient(dquery_ref[...], src_row, rel_col, rel_ref, rows)
    update(emb_ref, state_ref, gradient, new_ref, new_state_ref)


def loss_tail(total):
    total = total[0:1, :]
    high = total.astype(BF).astype(F32)
    rest = total - high
    mid = rest.astype(BF).astype(F32)
    return put_rows((PAD, total.shape[1]), [high, mid, rest - mid]).astype(BF)


def loss_of(tail):
    tail = tail.astype(F32)
    return (tail[0:1, :] + tail[1:2, :]) + tail[2:3, :]


def halve_kernel(with_loss, final, stage, came_ref, keep_ref, *refs):
    base = PAD if with_loss else 0
    if with_loss:
        loss_in, *refs = refs
    if final:
        give_ref, *refs = refs
    else:
        give_ref, next_ref, *refs = refs
    count = keep_ref.shape[0]
    half = count // 2
    if with_loss:
        (loss_out,) = refs
        total = loss_in[...] + loss_of(came_ref[0:PAD, :])
        loss_out[...] = total
        give_ref[0:PAD, :] = loss_tail(total)
    total = keep_ref[...] + came_ref[base : base + count, :].astype(F32)
    if final:
        give_ref[base : base + count, :] = total.astype(BF)
    else:
        upper = stage.upper() == 1
        next_ref[...] = jnp.where(upper, total[half:], total[:half])
        give_ref[base : base + half, :] = jnp.where(upper, total[:half], total[half:]).astype(BF)


def meet_kernel(with_loss, came_ref, mine_ref, *refs):
    base = PAD if with_loss else 0
    if with_loss:
        loss_in, out_ref, loss_out = refs
        loss_out[...] = loss_in[...] + loss_of(came_ref[0:PAD, :])
    else:
        (out_ref,) = refs
    count = out_ref.shape[0]
    total = came_ref[base : base + count, :].astype(F32) + mine_ref[base : base + count, :].astype(F32)
    out_ref[...] = total.astype(BF)


def join_kernel(stage, mine_ref, came_ref, out_ref):
    half = mine_ref.shape[0]
    upper = stage.upper() == 1
    mine, came = mine_ref[...], came_ref[...]
    out_ref[0:half, :] = jnp.where(upper, came, mine)
    out_ref[half : 2 * half, :] = jnp.where(upper, mine, came)


def spread_kernel(stage, *refs):
    out_ref = refs[-1]
    k = pl.program_id(0)
    upper = stage.upper()
    for n in range(len(refs) // 2):
        mine_ref, came_ref = refs[2 * n], refs[2 * n + 1]

        @pl.when(k == 2 * n + upper)
        def _(mine_ref=mine_ref):
            out_ref[0] = mine_ref[...].astype(F32)

        @pl.when(k == 2 * n + 1 - upper)
        def _(came_ref=came_ref):
            out_ref[0] = came_ref[...].astype(F32)


def xor_route(axis, mask):
    return [(low, low ^ mask) for low in range(lax.axis_size(axis))]


class Stage:
    def __init__(self, axis, even_bit, odd_bit):
        self.axis, self.even_bit, self.odd_bit = axis, even_bit, odd_bit
        self.route = [
            (n, n ^ (1 << (odd_bit if n & 1 else even_bit))) for n in range(lax.axis_size(axis))
        ]

    def upper(self):
        me = lax.axis_index(self.axis)
        even = jnp.bitwise_and(jnp.right_shift(me, self.even_bit), 1)
        if self.even_bit == self.odd_bit:
            return even
        odd = jnp.bitwise_and(jnp.right_shift(me, self.odd_bit), 1)
        return jnp.where(jnp.bitwise_and(me, 1) == 1, odd, even)

    def swap(self, block):
        return lax.ppermute(block, self.axis, self.route)


def make_stages():
    bits_d = lax.axis_size("dom").bit_length() - 1
    bits_g = lax.axis_size("grp").bit_length() - 1
    up = list(range(1, bits_d))
    stages = [Stage("dom", 0, 0)]
    stages += [Stage("dom", a, b) for a, b in zip(up, up[::-1])]
    stages += [Stage("grp", bit, bit) for bit in range(bits_g)]
    return stages


def halve(stage, came, keep, loss, final):
    with_loss = loss is not None
    count, width = keep.shape
    base = PAD if with_loss else 0
    sent = count if final else count // 2
    if sent % ROW_BLOCK:
        total = keep + came[base:].astype(F32)
        if with_loss:
            loss = loss + loss_of(came[:PAD])
        if final:
            give, rest = total.astype(BF), None
        else:
            upper = stage.upper() == 1
            give = jnp.where(upper, total[:sent], total[sent:]).astype(BF)
            rest = jnp.where(upper, total[sent:], total[:sent])
        if with_loss:
            give = jnp.concatenate([loss_tail(loss), give])
        return give, rest, loss
    outs = [((base + sent, width), BF)]
    if not final:
        outs.append(((sent, width), F32))
    args = [came, keep]
    if with_loss:
        outs.append((loss.shape, F32))
        args.append(loss)
    got = list(
        call(functools.partial(halve_kernel, with_loss, final, stage), outs, args, name="halve")
    )
    give = got.pop(0)
    rest = None if final else got.pop(0)
    return give, rest, (got.pop(0) if with_loss else None)


def meet(came, mine, loss):
    with_loss = loss is not None
    base = PAD if with_loss else 0
    count, width = mine.shape[0] - base, mine.shape[1]
    if count % ROW_BLOCK:
        total = (came[base:].astype(F32) + mine[base:].astype(F32)).astype(BF)
        return total, (loss + loss_of(came[:PAD]) if with_loss else None)
    outs, args = [((count, width), BF)], [came, mine]
    if with_loss:
        outs.append((loss.shape, F32))
        args.append(loss)
    got = call(functools.partial(meet_kernel, with_loss), outs, args, name="meet")
    return got[0], (got[1] if with_loss else None)


def join(stage, mine, came):
    half, width = mine.shape
    if half % ROW_BLOCK:
        upper = stage.upper() == 1
        return jnp.concatenate([jnp.where(upper, came, mine), jnp.where(upper, mine, came)])
    (out,) = call(
        functools.partial(join_kernel, stage), [((2 * half, width), BF)], [mine, came], name="join"
    )
    return out


def all_sum(stages, gives, keeps, loss):
    losses = [loss] + [None] * (len(gives) - 1)
    gives, keeps = list(gives), list(keeps)
    streams = range(len(gives))
    for at, stage in enumerate(stages[:-1]):
        final = at == len(stages) - 2
        for n in streams:
            came = stage.swap(gives[n])
            gives[n], keeps[n], losses[n] = halve(
                stages[at + 1], came, keeps[n], losses[n], final
            )
    values = [None] * len(gives)
    for n in streams:
        came = stages[-1].swap(gives[n])
        values[n], losses[n] = meet(came, gives[n], losses[n])
    for stage in stages[-2:0:-1]:
        for n in streams:
            came = stage.swap(values[n])
            values[n] = join(stage, values[n], came)
    pairs = []
    for n in streams:
        pairs += [values[n], stages[0].swap(values[n])]
    rows, width = values[0].shape
    count = 2 * len(gives)
    total = pl.pallas_call(
        functools.partial(spread_kernel, stages[0]),
        grid=(count,),
        out_shape=jax.ShapeDtypeStruct((count, rows, width), F32),
        in_specs=[pl.BlockSpec(memory_space=pltpu.VMEM)] * count,
        out_specs=pl.BlockSpec((1, rows, width), lambda k: (k, 0, 0)),
        compiler_params=pltpu.CompilerParams(vmem_limit_bytes=8 << 20),
        name="spread",
    )(*pairs)
    return total, losses[0][0, 0]


def exchange(block, axis, mask, beside):
    bits = lax.axis_size(axis).bit_length() - 1
    done = 0
    extra = None
    while done < bits:
        width = min(DIGIT, bits - done)
        digit = jnp.bitwise_and(jnp.right_shift(mask, done), (1 << width) - 1)
        last = done + width >= bits
        branches = []
        for value in range(1 << width):

            def branch(x, value=value, done=done, last=last):
                if value:
                    x = lax.ppermute(x, axis, xor_route(axis, value << done))
                return (x, beside()) if last else x

            if value or done or not last:
                branches.append(branch)
        if done == 0 and last:
            digit = digit - 1
        got = lax.switch(digit, branches, block)
        block, extra = got if last else (got, None)
        done += width
    return block, extra


def body(embeddings, ada_state, relations, plan, src_rows, dst_rows, rel_ids):
    rows, width = embeddings.shape[1:]
    count = relations.shape[0]
    edges = src_rows.shape[-1]
    emb = embeddings[0]
    src, dst, rid = src_rows[0, 0], dst_rows[0, 0], rel_ids[0, 0]
    square = 2 * rows * width * edges
    stages = make_stages()
    packed = ((rows + PAD, width), BF)
    edge_b = ((edges, width), BF)
    edge_t = ((width, edges), BF)
    part = (relations.shape, F32)
    line = ((8, width), F32)

    (own,) = call(pack_kernel, [packed], [emb, src, dst, rid], name="pack")
    pair, (rel_b, query, src_t) = exchange(
        own,
        "dom",
        plan[0],
        lambda: tuple(
            call(
                first_query_kernel,
                [(relations.shape, BF), edge_b, edge_t],
                [own, relations, src, rid],
                flops=5 * square,
                name="query",
                room=6 << 20,
            )
        ),
    )
    new, own_next, state, dquery, loss = call(
        functools.partial(round_kernel, 0),
        [((rows, width), F32), packed, ((1, rows), F32), edge_b, line],
        [pair, own, emb, ada_state, query, rel_b, src, dst, rid],
        flops=14 * square,
        name="round",
        room=12 << 20,
    )
    pair, (query, src_t, rel_part) = exchange(
        own_next,
        "dom",
        plan[1],
        lambda: tuple(
            call(
                functools.partial(next_query_kernel, 1),
                [edge_b, edge_t, part],
                [own_next, rel_b, src, rid, src_t, dquery],
                flops=9 * square,
                name="query",
                room=6 << 20,
            )
        ),
    )
    halves = count // 2
    dquery, loss, *gives = call(
        functools.partial(last_own_kernel, 1, stages[0]),
        [edge_b, line] + [((PAD + width, width), BF)] + [((width, width), BF)] * (halves - 1),
        [pair, query, src_t, dst, rid, rel_part, loss],
        flops=4 * square,
        name="own",
        room=8 << 20,
    )
    keeps = call(
        functools.partial(keep_kernel, 1, stages[0]),
        [((width, width), F32)] * halves,
        [src_t, dquery, rid, rel_part],
        flops=2 * square,
        name="keep",
        room=4 << 20,
    )
    new, state = call(
        functools.partial(last_rows_kernel, 1),
        [((rows, width), F32), ((1, rows), F32)],
        [pair, own_next, new, state, dquery, rel_b, src, rid],
        flops=12 * square,
        name="rows",
        room=10 << 20,
    )
    rel_total, loss_total = all_sum(stages, gives, keeps, loss)
    mean_loss = loss_total / (lax.axis_size("dom") * lax.axis_size("grp") * ROUNDS * EDGES)
    return (new[None], state, rel_total, mean_loss)


def solution(mesh):
    return jax.shard_map(
        body,
        mesh=mesh,
        in_specs=(
            P("grp", "dom", None),
            P("grp", "dom"),
            P(),
            P(),
            P("grp", "dom", None, None),
            P("grp", "dom", None, None),
            P("grp", "dom", None, None),
        ),
        out_specs=(P("grp", "dom", None), P("grp", "dom"), P(), P()),
        check_vma=False,
    )
```

time: 283 us -> 111 us (0.39)
  waiting for transfers between devices: 141 us -> 33.1 us
  blocking collectives: 47.6 us -> 0 us
  Pallas kernels: 0 us -> 40.3 us
  other arithmetic: 24 us -> 0 us
  matrix products: 23.4 us -> 0 us
  between operations: 21.5 us -> 3.95 us
  starting transfers between devices: 14.2 us -> 30.2 us
  local copies, waits for them, and re-layouts: 10.4 us -> 3.78 us
    psum x1 -> x0, waiting for transfers between devices: 67.8 us -> none  [body(): rel_total, loss_total = lax.psum((rel_sum, loss_sum), ('dom', 'grp'))]
    psum x1 -> x0, blocking collectives: 47.6 us -> none  [body(): rel_total, loss_total = lax.psum((rel_sum, loss_sum), ('dom', 'grp'))]
    pallas_call x0 -> x24, Pallas kernels: none -> 40.3 us  [the longest x23 37.8 us: call(): pl.pallas_call(kernel, out_shape=[jax.ShapeDtypeStruct(s, d) for s, d in...]
    ppermute x12 -> x20, waiting for transfers between devices: 73.1 us -> 33.1 us  [the longest x18 22.7 us: swap(): return lax.ppermute(block, self.axis, self.route)]
    dot_general x12 -> x0, matrix products: 23.4 us -> none  [the longest x2 5.7 us: apply_back(): jnp.einsum('ef,kdf->ked', dquery, rel_b, preferred_element_type=jnp.float32)]
    ppermute x12 -> x20, starting transfers between devices: 14.2 us -> 30.2 us  [the longest x18 23.3 us: swap(): return lax.ppermute(block, self.axis, self.route)]
    scatter-add x2 -> x0, other arithmetic: 9.51 us -> none  [apply_back(): jnp.zeros((row_count, src_grad.shape[1]), jnp.float32).at[src_idx]]
    convert_element_type x7 -> x0, other arithmetic: 6.61 us -> none  [the longest x1 3.78 us: body(): rel_b = relations.astype(jnp.bfloat16)]
  transfers between devices with their start and end apart: 13 -> 20, of which waited for: 10 -> 14; matrix products, arithmetic and copies ran while one was open for 14% -> 0% of each run, Pallas kernels for 0% -> 22%
where the time goes in v2:
time: 111 us
  Pallas kernels  40.3 us (36%)
  waiting for transfers between devices  33.1 us (30%)
  starting transfers between devices  30.2 us (27%)
  between operations  3.95 us (4%)
  local copies, waits for them, and re-layouts  3.78 us (3%)
    pallas_call x23, Pallas kernels, call(): pl.pallas_call(kernel, out_shape=[jax.ShapeDtypeStruct(s, d) for s, d in...  37.8 us
    ppermute x18, starting transfers between devices, swap(): return lax.ppermute(block, self.axis, self.route)  23.3 us
    ppermute x18, waiting for transfers between devices, swap(): return lax.ppermute(block, self.axis, self.route)  22.7 us
    ppermute x2, waiting for transfers between devices, branch(): x = lax.ppermute(x, axis, xor_route(axis, value << done))  10.4 us
    ppermute x2, starting transfers between devices, branch(): x = lax.ppermute(x, axis, xor_route(axis, value << done))  6.95 us
    pallas_call x1, Pallas kernels, all_sum(): pl.pallas_call(functools.partial(spread_kernel, stages[0]), grid=(count,)...  2.48 us
  transfers between devices with their start and end apart: 20, of which 14 were waited for; matrix products, arithmetic and copies ran while one was open for 0% of the time, Pallas kernels for 22%

profile of v2, /device:TPU:0, one launch (start us, length us, event | category | flops | bytes accessed | tf_op | source)
XLA Modules:
  0.0 111.5 jit_solution(11000238432638287358)
XLA Ops:
  0.6 1.3 %fusion = (s32[1]{0:T(128)}, s32[1]{0:T(128)}) fusion(s32[2]{0:T(128)} %param.24), kind=kLoop, calls=%fused_computation | loop fusion | bytes 16 | tf_op jit(solution)/shard_map/slice | solution.py:535
  3.2 0.0 copy-start
  3.3 1.2 %copy-done = f32[1,512,512]{2,1,0:T(8,128)S(1)} copy-done((f32[1,512,512]{2,1,0:T(8,128)S(1)}, f32[1,512,512]{2,1,0:T(8,128)}, u32[]{:S(2)}) %copy-start) | copy-done | bytes 1048600
  4.5 0.7 copy-done.2
  5.2 0.8 pack.1.own_ref
  5.9 0.0 copy-start.1
  5.9 0.0 copy-start.3
  6.0 0.0 copy-start.4
  6.0 16.1 %conditional.2 = (bf16[528,512]{1,0:T(8,128)(2,1)}, bf16[4,512,512]{2,1,0:T(8,128)(2,1)}, bf16[512,512]{1,0:T(8,128)(2,1)S(1)}, bf16[512,512]{1,0:T(8,128)(2,1)}) conditional(s32[]{:T(128)} %bitcast.1, (bf16[528,512]{1,0:T(8,128)(2,1)S(1)}, f32[4,512,512]{2,1,0:T(8,128)}, s32[2,512]{1,0:T(2,128)}, ...), branch_computations={%region_0.0_spmd, %region_1.0_spmd, %region_2.0_spmd, %region_3.0_... | conditional | flops 1342177280 | bytes 10051656 | solution.py:511
  6.0 3.4 %collective-permute-start.6 = (bf16[528,512]{1,0:T(8,128)(2,1)S(1)}, bf16[528,512]{1,0:T(8,128)(2,1)}, u32[]{:S(2)}, u32[]{:S(2)}) collective-permute-start(bf16[528,512]{1,0:T(8,128)(2,1)S(1)} %get-tuple-element.182.own_ref), channel_id=1, source_target_pairs={{0,28},{4,24},{8,20},{12,16},{16,12},{20,8},{24,4},{28,0},{1,29},{... | collective-permute-start | bytes 1622024 | tf_op jit(solution)/shard_map/cond/branch_6_fun/ppermute | solution.py:504
  9.4 6.6 %query.20 = (bf16[4,512,512]{2,1,0:T(8,128)(2,1)}, bf16[512,512]{1,0:T(8,128)(2,1)S(1)}, bf16[512,512]{1,0:T(8,128)(2,1)}) custom-call(bf16[528,512]{1,0:T(8,128)(2,1)S(1)} %get-tuple-element.182.own_ref, f32[4,512,512]{2,1,0:T(8,128)} %get-tuple-element.183.rel_in_ref, s32[2,512]{1,0:T(2,128)} %get-tuple-element.184.src_ref, ...), custom_call_target="tpu_custom_call" | custom-call | flops 1342177280 | bytes 7888896 | tf_op jit(solution)/shard_map/cond/branch_6_fun/query/pallas_call | solution.py:37
  16.0 6.1 %collective-permute-done.6 = bf16[528,512]{1,0:T(8,128)(2,1)} collective-permute-done((bf16[528,512]{1,0:T(8,128)(2,1)S(1)}, bf16[528,512]{1,0:T(8,128)(2,1)}, u32[]{:S(2)}, u32[]{:S(2)}) %collective-permute-start.6) | collective-permute-done | bytes 540704 | tf_op jit(solution)/shard_map/cond/branch_6_fun/ppermute | solution.py:504
  22.1 0.0 copy-start.6
  22.1 0.0 copy-start.7
  22.2 0.0 copy-start.10
  22.2 8.4 %round.1 = (f32[512,512]{1,0:T(8,128)S(1)}, bf16[528,512]{1,0:T(8,128)(2,1)}, f32[1,512]{1,0:T(1,128)S(1)}, bf16[512,512]{1,0:T(8,128)(2,1)S(1)}, f32[8,512]{1,0:T(8,128)S(1)}) custom-call(bf16[528,512]{1,0:T(8,128)(2,1)} %get-tuple-element.296.pair_ref, bf16[528,512]{1,0:T(8,128)(2,1)S(1)} %pack.1.own_ref, f32[512,512]{1,0:T(8,128)S(1)} %bitcast.9, ...), custom_call_target="tpu_custom_call" | custom-call | flops 3758096384 | bytes 6897664 | tf_op jit(solution)/shard_map/round/pallas_call | solution.py:37
  30.6 16.4 %conditional.3 = (bf16[528,512]{1,0:T(8,128)(2,1)}, bf16[512,512]{1,0:T(8,128)(2,1)S(1)}, bf16[512,512]{1,0:T(8,128)(2,1)S(1)}, f32[4,512,512]{2,1,0:T(8,128)}) conditional(s32[]{:T(128)} %bitcast, (bf16[528,512]{1,0:T(8,128)(2,1)}, bf16[4,512,512]{2,1,0:T(8,128)(2,1)S(1)}, s32[2,512]{1,0:T(2,128)S(1)}, ...), branch_computations={%region_7.0_spmd, %region_8.0_spmd, %region_9.0_spmd, %region_10.0... | conditional | flops 2415919104 | bytes 11100232 | solution.py:511
  30.6 3.5 %collective-permute-start.12 = (bf16[528,512]{1,0:T(8,128)(2,1)}, bf16[528,512]{1,0:T(8,128)(2,1)}, u32[]{:S(2)}, u32[]{:S(2)}) collective-permute-start(bf16[528,512]{1,0:T(8,128)(2,1)} %get-tuple-element.234.own_ref), channel_id=1, source_target_pairs={{0,24},{4,28},{8,16},{12,20},{16,8},{20,12},{24,0},{28,4},{1,25},{... | collective-permute-start | bytes 1622024 | tf_op jit(solution)/shard_map/cond/branch_5_fun/ppermute | solution.py:504
  34.2 8.5 %query.26 = (bf16[512,512]{1,0:T(8,128)(2,1)S(1)}, bf16[512,512]{1,0:T(8,128)(2,1)S(1)}, f32[4,512,512]{2,1,0:T(8,128)}) custom-call(bf16[528,512]{1,0:T(8,128)(2,1)} %get-tuple-element.234.own_ref, bf16[4,512,512]{2,1,0:T(8,128)(2,1)S(1)} %get-tuple-element.235.rel_ref, s32[2,512]{1,0:T(2,128)S(1)} %get-tuple-element.236.src_ref, ...), custom_call_target="tpu_custom_call" | custom-call | flops 2415919104 | bytes 8937472 | tf_op jit(solution)/shard_map/cond/branch_5_fun/query/pallas_call | solution.py:37
  42.7 4.4 %collective-permute-done.12 = bf16[528,512]{1,0:T(8,128)(2,1)} collective-permute-done((bf16[528,512]{1,0:T(8,128)(2,1)}, bf16[528,512]{1,0:T(8,128)(2,1)}, u32[]{:S(2)}, u32[]{:S(2)}) %collective-permute-start.12) | collective-permute-done | bytes 540704 | tf_op jit(solution)/shard_map/cond/branch_5_fun/ppermute | solution.py:504
  47.0 4.4 %own.1 = (bf16[512,512]{1,0:T(8,128)(2,1)S(1)}, f32[8,512]{1,0:T(8,128)S(1)}, bf16[528,512]{1,0:T(8,128)(2,1)S(1)}, bf16[512,512]{1,0:T(8,128)(2,1)S(1)}) custom-call(bf16[528,512]{1,0:T(8,128)(2,1)} %get-tuple-element.302.pair_ref, bf16[512,512]{1,0:T(8,128)(2,1)S(1)} %get-tuple-element.305.query_ref, bf16[512,512]{1,0:T(8,128)(2,1)S(1)} %get-tuple-element.306.src_t_ref, ...), custom_call_target="tpu_custom_call" | custom-call | flops 1073741824 | bytes 7413760 | tf_op jit(solution)/shard_map/own/pallas_call | solution.py:37
  51.5 0.1 collective-permute-start.14
  51.6 0.5 collective-permute-start.23
  52.1 1.0 keep.1
  53.1 0.4 collective-permute-done.14.came_ref
  53.5 0.1 halve.8
  53.6 1.7 %collective-permute-start.15 = (bf16[272,512]{1,0:T(8,128)(2,1)S(1)}, bf16[272,512]{1,0:T(8,128)(2,1)S(1)}, u32[]{:S(2)}, u32[]{:S(2)}) collective-permute-start(bf16[272,512]{1,0:T(8,128)(2,1)S(1)} %get-tuple-element.315), channel_id=1, source_target_pairs={{0,8},{4,20},{8,0},{12,28},{16,24},{20,4},{24,16},{28,12},{1,9},{5... | collective-permute-start | bytes 835592 | tf_op jit(solution)/shard_map/ppermute | solution.py:383
  55.4 0.0 collective-permute-done.23.came_ref
  55.4 0.2 halve.12
  55.5 0.6 collective-permute-start.24
  56.1 4.1 %collective-permute-done.15.came_ref = bf16[272,512]{1,0:T(8,128)(2,1)S(1)} collective-permute-done((bf16[272,512]{1,0:T(8,128)(2,1)S(1)}, bf16[272,512]{1,0:T(8,128)(2,1)S(1)}, u32[]{:S(2)}, u32[]{:S(2)}) %collective-permute-start.15) | collective-permute-done | bytes 278560 | tf_op jit(solution)/shard_map/ppermute | solution.py:383
  60.3 0.1 halve.9
  60.4 1.8 %collective-permute-start.16 = (bf16[144,512]{1,0:T(8,128)(2,1)S(1)}, bf16[144,512]{1,0:T(8,128)(2,1)S(1)}, u32[]{:S(2)}, u32[]{:S(2)}) collective-permute-start(bf16[144,512]{1,0:T(8,128)(2,1)S(1)} %get-tuple-element.318), channel_id=1, source_target_pairs={{0,16},{4,12},{8,24},{12,4},{16,0},{20,28},{24,8},{28,20},{1,17},{... | collective-permute-start | bytes 442376 | tf_op jit(solution)/shard_map/ppermute | solution.py:383
  62.1 1.7 %collective-permute-done.24.came_ref = bf16[256,512]{1,0:T(8,128)(2,1)S(1)} collective-permute-done((bf16[256,512]{1,0:T(8,128)(2,1)S(1)}, bf16[256,512]{1,0:T(8,128)(2,1)S(1)}, u32[]{:S(2)}, u32[]{:S(2)}) %collective-permute-start.24) | collective-permute-done | bytes 262176 | tf_op jit(solution)/shard_map/ppermute | solution.py:383
  63.8 0.1 halve.13
  63.9 1.8 %collective-permute-start.25 = (bf16[128,512]{1,0:T(8,128)(2,1)S(1)}, bf16[128,512]{1,0:T(8,128)(2,1)S(1)}, u32[]{:S(2)}, u32[]{:S(2)}) collective-permute-start(bf16[128,512]{1,0:T(8,128)(2,1)S(1)} %get-tuple-element.331), channel_id=1, source_target_pairs={{0,16},{4,12},{8,24},{12,4},{16,0},{20,28},{24,8},{28,20},{1,17},{... | collective-permute-start | bytes 393224 | tf_op jit(solution)/shard_map/ppermute | solution.py:383
  65.7 0.1 halve.10
  65.8 1.6 %collective-permute-start.17 = (bf16[80,512]{1,0:T(8,128)(2,1)S(1)}, bf16[80,512]{1,0:T(8,128)(2,1)S(1)}, u32[]{:S(2)}, u32[]{:S(2)}) collective-permute-start(bf16[80,512]{1,0:T(8,128)(2,1)S(1)} %get-tuple-element.321), channel_id=1, source_target_pairs={{0,1},{1,0},{2,3},{3,2},{4,5},{5,4},{6,7},{7,6},{8,9},{9,8},{10,11... | collective-permute-start | bytes 245768 | tf_op jit(solution)/shard_map/ppermute | solution.py:383
  67.4 1.6 %collective-permute-done.25.came_ref = bf16[128,512]{1,0:T(8,128)(2,1)S(1)} collective-permute-done((bf16[128,512]{1,0:T(8,128)(2,1)S(1)}, bf16[128,512]{1,0:T(8,128)(2,1)S(1)}, u32[]{:S(2)}, u32[]{:S(2)}) %collective-permute-start.25) | collective-permute-done | bytes 131104 | tf_op jit(solution)/shard_map/ppermute | solution.py:383
  69.0 1.7 %collective-permute-start.26 = (bf16[64,512]{1,0:T(8,128)(2,1)S(1)}, bf16[64,512]{1,0:T(8,128)(2,1)S(1)}, u32[]{:S(2)}, u32[]{:S(2)}) collective-permute-start(bf16[64,512]{1,0:T(8,128)(2,1)S(1)} %get-tuple-element.333), channel_id=1, source_target_pairs={{0,1},{1,0},{2,3},{3,2},{4,5},{5,4},{6,7},{7,6},{8,9},{9,8},{10,11... | collective-permute-start | bytes 196616 | tf_op jit(solution)/shard_map/ppermute | solution.py:383
  70.7 0.0 collective-permute-done.17.came_ref
  70.8 2.7 %collective-permute-start.18 = (bf16[80,512]{1,0:T(8,128)(2,1)S(1)}, bf16[80,512]{1,0:T(8,128)(2,1)S(1)}, u32[]{:S(2)}, u32[]{:S(2)}) collective-permute-start(bf16[80,512]{1,0:T(8,128)(2,1)S(1)} %get-tuple-element.324.mine_ref), channel_id=1, source_target_pairs={{0,2},{1,3},{2,0},{3,1},{4,6},{5,7},{6,4},{7,5},{8,10},{9,11},{10,... | collective-permute-start | bytes 245768 | tf_op jit(solution)/shard_map/ppermute | solution.py:383
  73.4 0.3 collective-permute-done.26.came_ref
  73.7 2.4 %collective-permute-start.27 = (bf16[64,512]{1,0:T(8,128)(2,1)S(1)}, bf16[64,512]{1,0:T(8,128)(2,1)S(1)}, u32[]{:S(2)}, u32[]{:S(2)}) collective-permute-start(bf16[64,512]{1,0:T(8,128)(2,1)S(1)} %halve.15.mine_ref), channel_id=1, source_target_pairs={{0,2},{1,3},{2,0},{3,1},{4,6},{5,7},{6,4},{7,5},{8,10},{9,11},{10,... | collective-permute-start | bytes 196616 | tf_op jit(solution)/shard_map/ppermute | solution.py:383
  76.1 2.9 %collective-permute-done.27.came_ref = bf16[64,512]{1,0:T(8,128)(2,1)S(1)} collective-permute-done((bf16[64,512]{1,0:T(8,128)(2,1)S(1)}, bf16[64,512]{1,0:T(8,128)(2,1)S(1)}, u32[]{:S(2)}, u32[]{:S(2)}) %collective-permute-start.27) | collective-permute-done | bytes 65568 | tf_op jit(solution)/shard_map/ppermute | solution.py:383
  79.1 2.2 %collective-permute-start.28 = (bf16[64,512]{1,0:T(8,128)(2,1)S(1)}, bf16[64,512]{1,0:T(8,128)(2,1)S(1)}, u32[]{:S(2)}, u32[]{:S(2)}) collective-permute-start(bf16[64,512]{1,0:T(8,128)(2,1)S(1)} %meet.3.mine_ref), channel_id=1, source_target_pairs={{0,1},{1,0},{2,3},{3,2},{4,5},{5,4},{6,7},{7,6},{8,9},{9,8},{10,11... | collective-permute-start | bytes 196616 | tf_op jit(solution)/shard_map/ppermute | solution.py:383
  81.3 0.1 collective-permute-start.19
  81.4 2.1 %collective-permute-done.28.came_ref = bf16[64,512]{1,0:T(8,128)(2,1)S(1)} collective-permute-done((bf16[64,512]{1,0:T(8,128)(2,1)S(1)}, bf16[64,512]{1,0:T(8,128)(2,1)S(1)}, u32[]{:S(2)}, u32[]{:S(2)}) %collective-permute-start.28) | collective-permute-done | bytes 65568 | tf_op jit(solution)/shard_map/ppermute | solution.py:383
  83.6 1.6 %collective-permute-start.29 = (bf16[128,512]{1,0:T(8,128)(2,1)S(1)}, bf16[128,512]{1,0:T(8,128)(2,1)S(1)}, u32[]{:S(2)}, u32[]{:S(2)}) collective-permute-start(bf16[128,512]{1,0:T(8,128)(2,1)S(1)} %join.9.mine_ref), channel_id=1, source_target_pairs={{0,16},{4,12},{8,24},{12,4},{16,0},{20,28},{24,8},{28,20},{1,17},{... | collective-permute-start | bytes 393224 | tf_op jit(solution)/shard_map/ppermute | solution.py:383
  85.1 0.5 collective-permute-done.19.came_ref
  85.7 1.3 %collective-permute-start.20 = (bf16[128,512]{1,0:T(8,128)(2,1)S(1)}, bf16[128,512]{1,0:T(8,128)(2,1)S(1)}, u32[]{:S(2)}, u32[]{:S(2)}) collective-permute-start(bf16[128,512]{1,0:T(8,128)(2,1)S(1)} %join.6.mine_ref), channel_id=1, source_target_pairs={{0,16},{4,12},{8,24},{12,4},{16,0},{20,28},{24,8},{28,20},{1,17},{... | collective-permute-start | bytes 393224 | tf_op jit(solution)/shard_map/ppermute | solution.py:383
  87.0 3.0 %collective-permute-done.29.came_ref = bf16[128,512]{1,0:T(8,128)(2,1)S(1)} collective-permute-done((bf16[128,512]{1,0:T(8,128)(2,1)S(1)}, bf16[128,512]{1,0:T(8,128)(2,1)S(1)}, u32[]{:S(2)}, u32[]{:S(2)}) %collective-permute-start.29) | collective-permute-done | bytes 131104 | tf_op jit(solution)/shard_map/ppermute | solution.py:383
  90.0 1.5 %collective-permute-start.30 = (bf16[256,512]{1,0:T(8,128)(2,1)S(1)}, bf16[256,512]{1,0:T(8,128)(2,1)S(1)}, u32[]{:S(2)}, u32[]{:S(2)}) collective-permute-start(bf16[256,512]{1,0:T(8,128)(2,1)S(1)} %join.10.mine_ref), channel_id=1, source_target_pairs={{0,8},{4,20},{8,0},{12,28},{16,24},{20,4},{24,16},{28,12},{1,9},{5... | collective-permute-start | bytes 786440 | tf_op jit(solution)/shard_map/ppermute | solution.py:383
  91.6 1.2 %collective-permute-done.20.came_ref = bf16[128,512]{1,0:T(8,128)(2,1)S(1)} collective-permute-done((bf16[128,512]{1,0:T(8,128)(2,1)S(1)}, bf16[128,512]{1,0:T(8,128)(2,1)S(1)}, u32[]{:S(2)}, u32[]{:S(2)}) %collective-permute-start.20) | collective-permute-done | bytes 131104 | tf_op jit(solution)/shard_map/ppermute | solution.py:383
  92.9 1.5 %collective-permute-start.21 = (bf16[256,512]{1,0:T(8,128)(2,1)S(1)}, bf16[256,512]{1,0:T(8,128)(2,1)S(1)}, u32[]{:S(2)}, u32[]{:S(2)}) collective-permute-start(bf16[256,512]{1,0:T(8,128)(2,1)S(1)} %join.7.mine_ref), channel_id=1, source_target_pairs={{0,8},{4,20},{8,0},{12,28},{16,24},{20,4},{24,16},{28,12},{1,9},{5... | collective-permute-start | bytes 786440 | tf_op jit(solution)/shard_map/ppermute | solution.py:383
  94.4 2.1 %collective-permute-done.30.came_ref = bf16[256,512]{1,0:T(8,128)(2,1)S(1)} collective-permute-done((bf16[256,512]{1,0:T(8,128)(2,1)S(1)}, bf16[256,512]{1,0:T(8,128)(2,1)S(1)}, u32[]{:S(2)}, u32[]{:S(2)}) %collective-permute-start.30) | collective-permute-done | bytes 262176 | tf_op jit(solution)/shard_map/ppermute | solution.py:383
  96.5 0.1 join.11.refs_2_
  96.6 0.1 collective-permute-start.31
  96.6 2.7 %collective-permute-done.21.came_ref = bf16[256,512]{1,0:T(8,128)(2,1)S(1)} collective-permute-done((bf16[256,512]{1,0:T(8,128)(2,1)S(1)}, bf16[256,512]{1,0:T(8,128)(2,1)S(1)}, u32[]{:S(2)}, u32[]{:S(2)}) %collective-permute-start.21) | collective-permute-done | bytes 262176 | tf_op jit(solution)/shard_map/ppermute | solution.py:383
  99.3 0.1 join.8.refs_0_
  99.4 0.1 collective-permute-start.22
  99.4 7.2 %rows.1 = (f32[512,512]{1,0:T(8,128)}, f32[1,512]{1,0:T(1,128)}) custom-call(bf16[528,512]{1,0:T(8,128)(2,1)} %get-tuple-element.302.pair_ref, bf16[528,512]{1,0:T(8,128)(2,1)} %get-tuple-element.299.own_ref, f32[512,512]{1,0:T(8,128)S(1)} %get-tuple-element.303.emb_ref, f32[1,512]{1,0:T(1,128)S(1)} %get-tuple-element.304.state_ref, ...), custom_call_target="tpu_custom_call" | custom-call | flops 3221225472 | bytes 5812224 | tf_op jit(solution)/shard_map/rows/pallas_call | solution.py:37
  106.7 0.5 slice.11
  107.8 2.5 %spread.1 = f32[4,512,512]{2,1,0:T(8,128)} custom-call(bf16[512,512]{1,0:T(8,128)(2,1)S(1)} %join.8.refs_0_, bf16[512,512]{1,0:T(8,128)(2,1)S(1)} %collective-permute-done.22.refs_1_, bf16[512,512]{1,0:T(8,128)(2,1)S(1)} %join.11.refs_2_, bf16[512,512]{1,0:T(8,128)(2,1)S(1)} %collective-permute-done.31.refs_3_), custom_call_target="tpu_custom_call" | custom-call | tf_op jit(solution)/shard_map/spread/pallas_call | solution.py:479
  (26 shorter events, 0.2 us)
Async XLA Ops:
  3.2 1.2 %copy-start = (f32[1,512,512]{2,1,0:T(8,128)S(1)}, f32[1,512,512]{2,1,0:T(8,128)}, u32[]{:S(2)}) copy-start(f32[1,512,512]{2,1,0:T(8,128)} %param.21) | copy-start | bytes 3145732
  4.5 0.7 copy-start.2
  5.9 16.2 %copy-start.1 = (f32[1,512,512]{2,1,0:T(8,128)S(1)}, f32[1,512,512]{2,1,0:T(8,128)}, u32[]{:S(2)}) copy-start(f32[1,512,512]{2,1,0:T(8,128)} %param.21) | copy-start | bytes 3145732
  5.9 16.2 %copy-start.3 = (s32[1,1,2,512]{3,2,1,0:T(2,128)S(1)}, s32[1,1,2,512]{3,2,1,0:T(2,128)}, u32[]{:S(2)}) copy-start(s32[1,1,2,512]{3,2,1,0:T(2,128)} %param.26) | copy-start | bytes 12292
  6.0 16.2 %copy-start.4 = (f32[1,512]{1,0:T(1,128)S(1)}, f32[1,512]{1,0:T(1,128)}, u32[]{:S(2)}) copy-start(f32[1,512]{1,0:T(1,128)} %state_ref.1) | copy-start | bytes 6148
  6.0 16.1 %collective-permute-start.6 = (bf16[528,512]{1,0:T(8,128)(2,1)S(1)}, bf16[528,512]{1,0:T(8,128)(2,1)}, u32[]{:S(2)}, u32[]{:S(2)}) collective-permute-start(bf16[528,512]{1,0:T(8,128)(2,1)S(1)} %get-tuple-element.182.own_ref), channel_id=1, source_target_pairs={{0,28},{4,24},{8,20},{12,16},{16,12},{20,8},{24,4},{28,0},{1,29},{... | collective-permute-start | bytes 1622024 | tf_op jit(solution)/shard_map/cond/branch_6_fun/ppermute | solution.py:504
  22.1 8.5 %copy-start.6 = (s32[1,1,2,512]{3,2,1,0:T(2,128)S(1)}, s32[1,1,2,512]{3,2,1,0:T(2,128)}, u32[]{:S(2)}) copy-start(s32[1,1,2,512]{3,2,1,0:T(2,128)} %param.27) | copy-start | bytes 12292
  22.1 8.5 %copy-start.7 = (s32[1,1,2,512]{3,2,1,0:T(2,128)S(1)}, s32[1,1,2,512]{3,2,1,0:T(2,128)}, u32[]{:S(2)}) copy-start(s32[1,1,2,512]{3,2,1,0:T(2,128)} %param.25) | copy-start | bytes 12292
  22.1 8.5 %copy-start.8 = (bf16[4,512,512]{2,1,0:T(8,128)(2,1)S(1)}, bf16[4,512,512]{2,1,0:T(8,128)(2,1)}, u32[]{:S(2)}) copy-start(bf16[4,512,512]{2,1,0:T(8,128)(2,1)} %get-tuple-element.298.rel_ref) | copy-start | bytes 6291460
  22.2 8.4 %copy-start.10 = (bf16[512,512]{1,0:T(8,128)(2,1)S(1)}, bf16[512,512]{1,0:T(8,128)(2,1)}, u32[]{:S(2)}) copy-start(bf16[512,512]{1,0:T(8,128)(2,1)} %get-tuple-element.300) | copy-start | bytes 1572868
  30.6 16.4 %collective-permute-start.12 = (bf16[528,512]{1,0:T(8,128)(2,1)}, bf16[528,512]{1,0:T(8,128)(2,1)}, u32[]{:S(2)}, u32[]{:S(2)}) collective-permute-start(bf16[528,512]{1,0:T(8,128)(2,1)} %get-tuple-element.234.own_ref), channel_id=1, source_target_pairs={{0,24},{4,28},{8,16},{12,20},{16,8},{20,12},{24,0},{28,4},{1,25},{... | collective-permute-start | bytes 1622024 | tf_op jit(solution)/shard_map/cond/branch_5_fun/ppermute | solution.py:504
  47.0 5.0 %copy-start.5 = (f32[4,512,512]{2,1,0:T(8,128)S(1)}, f32[4,512,512]{2,1,0:T(8,128)}, u32[]{:S(2)}) copy-start(f32[4,512,512]{2,1,0:T(8,128)} %get-tuple-element.307.part_ref) | copy-start | bytes 12582916
  51.5 2.0 %collective-permute-start.14 = (bf16[528,512]{1,0:T(8,128)(2,1)S(1)}, bf16[528,512]{1,0:T(8,128)(2,1)S(1)}, u32[]{:S(2)}, u32[]{:S(2)}) collective-permute-start(bf16[528,512]{1,0:T(8,128)(2,1)S(1)} %get-tuple-element.312), channel_id=1, source_target_pairs={{0,4},{4,0},{8,12},{12,8},{16,20},{20,16},{24,28},{28,24},{1,5},{5... | collective-permute-start | bytes 1622024 | tf_op jit(solution)/shard_map/ppermute | solution.py:383
  51.6 3.8 %collective-permute-start.23 = (bf16[512,512]{1,0:T(8,128)(2,1)S(1)}, bf16[512,512]{1,0:T(8,128)(2,1)S(1)}, u32[]{:S(2)}, u32[]{:S(2)}) collective-permute-start(bf16[512,512]{1,0:T(8,128)(2,1)S(1)} %get-tuple-element.327), channel_id=1, source_target_pairs={{0,4},{4,0},{8,12},{12,8},{16,20},{20,16},{24,28},{28,24},{1,5},{5... | collective-permute-start | bytes 1572872 | tf_op jit(solution)/shard_map/ppermute | solution.py:383
  53.6 6.6 %collective-permute-start.15 = (bf16[272,512]{1,0:T(8,128)(2,1)S(1)}, bf16[272,512]{1,0:T(8,128)(2,1)S(1)}, u32[]{:S(2)}, u32[]{:S(2)}) collective-permute-start(bf16[272,512]{1,0:T(8,128)(2,1)S(1)} %get-tuple-element.315), channel_id=1, source_target_pairs={{0,8},{4,20},{8,0},{12,28},{16,24},{20,4},{24,16},{28,12},{1,9},{5... | collective-permute-start | bytes 835592 | tf_op jit(solution)/shard_map/ppermute | solution.py:383
  55.4 44.0 %copy-start.9 = (bf16[4,512,512]{2,1,0:T(8,128)(2,1)S(1)}, bf16[4,512,512]{2,1,0:T(8,128)(2,1)}, u32[]{:S(2)}) copy-start(bf16[4,512,512]{2,1,0:T(8,128)(2,1)} %get-tuple-element.298.rel_ref) | copy-start | bytes 6291460
  55.5 8.3 %collective-permute-start.24 = (bf16[256,512]{1,0:T(8,128)(2,1)S(1)}, bf16[256,512]{1,0:T(8,128)(2,1)S(1)}, u32[]{:S(2)}, u32[]{:S(2)}) collective-permute-start(bf16[256,512]{1,0:T(8,128)(2,1)S(1)} %get-tuple-element.329), channel_id=1, source_target_pairs={{0,8},{4,20},{8,0},{12,28},{16,24},{20,4},{24,16},{28,12},{1,9},{5... | collective-permute-start | bytes 786440 | tf_op jit(solution)/shard_map/ppermute | solution.py:383
  60.4 5.3 %collective-permute-start.16 = (bf16[144,512]{1,0:T(8,128)(2,1)S(1)}, bf16[144,512]{1,0:T(8,128)(2,1)S(1)}, u32[]{:S(2)}, u32[]{:S(2)}) collective-permute-start(bf16[144,512]{1,0:T(8,128)(2,1)S(1)} %get-tuple-element.318), channel_id=1, source_target_pairs={{0,16},{4,12},{8,24},{12,4},{16,0},{20,28},{24,8},{28,20},{1,17},{... | collective-permute-start | bytes 442376 | tf_op jit(solution)/shard_map/ppermute | solution.py:383
  63.9 5.0 %collective-permute-start.25 = (bf16[128,512]{1,0:T(8,128)(2,1)S(1)}, bf16[128,512]{1,0:T(8,128)(2,1)S(1)}, u32[]{:S(2)}, u32[]{:S(2)}) collective-permute-start(bf16[128,512]{1,0:T(8,128)(2,1)S(1)} %get-tuple-element.331), channel_id=1, source_target_pairs={{0,16},{4,12},{8,24},{12,4},{16,0},{20,28},{24,8},{28,20},{1,17},{... | collective-permute-start | bytes 393224 | tf_op jit(solution)/shard_map/ppermute | solution.py:383
  65.8 5.0 %collective-permute-start.17 = (bf16[80,512]{1,0:T(8,128)(2,1)S(1)}, bf16[80,512]{1,0:T(8,128)(2,1)S(1)}, u32[]{:S(2)}, u32[]{:S(2)}) collective-permute-start(bf16[80,512]{1,0:T(8,128)(2,1)S(1)} %get-tuple-element.321), channel_id=1, source_target_pairs={{0,1},{1,0},{2,3},{3,2},{4,5},{5,4},{6,7},{7,6},{8,9},{9,8},{10,11... | collective-permute-start | bytes 245768 | tf_op jit(solution)/shard_map/ppermute | solution.py:383
  69.0 4.7 %collective-permute-start.26 = (bf16[64,512]{1,0:T(8,128)(2,1)S(1)}, bf16[64,512]{1,0:T(8,128)(2,1)S(1)}, u32[]{:S(2)}, u32[]{:S(2)}) collective-permute-start(bf16[64,512]{1,0:T(8,128)(2,1)S(1)} %get-tuple-element.333), channel_id=1, source_target_pairs={{0,1},{1,0},{2,3},{3,2},{4,5},{5,4},{6,7},{7,6},{8,9},{9,8},{10,11... | collective-permute-start | bytes 196616 | tf_op jit(solution)/shard_map/ppermute | solution.py:383
  70.8 10.6 %collective-permute-start.18 = (bf16[80,512]{1,0:T(8,128)(2,1)S(1)}, bf16[80,512]{1,0:T(8,128)(2,1)S(1)}, u32[]{:S(2)}, u32[]{:S(2)}) collective-permute-start(bf16[80,512]{1,0:T(8,128)(2,1)S(1)} %get-tuple-element.324.mine_ref), channel_id=1, source_target_pairs={{0,2},{1,3},{2,0},{3,1},{4,6},{5,7},{6,4},{7,5},{8,10},{9,11},{10,... | collective-permute-start | bytes 245768 | tf_op jit(solution)/shard_map/ppermute | solution.py:383
  73.7 5.3 %collective-permute-start.27 = (bf16[64,512]{1,0:T(8,128)(2,1)S(1)}, bf16[64,512]{1,0:T(8,128)(2,1)S(1)}, u32[]{:S(2)}, u32[]{:S(2)}) collective-permute-start(bf16[64,512]{1,0:T(8,128)(2,1)S(1)} %halve.15.mine_ref), channel_id=1, source_target_pairs={{0,2},{1,3},{2,0},{3,1},{4,6},{5,7},{6,4},{7,5},{8,10},{9,11},{10,... | collective-permute-start | bytes 196616 | tf_op jit(solution)/shard_map/ppermute | solution.py:383
  79.1 4.5 %collective-permute-start.28 = (bf16[64,512]{1,0:T(8,128)(2,1)S(1)}, bf16[64,512]{1,0:T(8,128)(2,1)S(1)}, u32[]{:S(2)}, u32[]{:S(2)}) collective-permute-start(bf16[64,512]{1,0:T(8,128)(2,1)S(1)} %meet.3.mine_ref), channel_id=1, source_target_pairs={{0,1},{1,0},{2,3},{3,2},{4,5},{5,4},{6,7},{7,6},{8,9},{9,8},{10,11... | collective-permute-start | bytes 196616 | tf_op jit(solution)/shard_map/ppermute | solution.py:383
  81.3 4.3 %collective-permute-start.19 = (bf16[64,512]{1,0:T(8,128)(2,1)S(1)}, bf16[64,512]{1,0:T(8,128)(2,1)S(1)}, u32[]{:S(2)}, u32[]{:S(2)}) collective-permute-start(bf16[64,512]{1,0:T(8,128)(2,1)S(1)} %get-tuple-element.326.mine_ref), channel_id=1, source_target_pairs={{0,1},{1,0},{2,3},{3,2},{4,5},{5,4},{6,7},{7,6},{8,9},{9,8},{10,11... | collective-permute-start | bytes 196616 | tf_op jit(solution)/shard_map/ppermute | solution.py:383
  83.6 6.4 %collective-permute-start.29 = (bf16[128,512]{1,0:T(8,128)(2,1)S(1)}, bf16[128,512]{1,0:T(8,128)(2,1)S(1)}, u32[]{:S(2)}, u32[]{:S(2)}) collective-permute-start(bf16[128,512]{1,0:T(8,128)(2,1)S(1)} %join.9.mine_ref), channel_id=1, source_target_pairs={{0,16},{4,12},{8,24},{12,4},{16,0},{20,28},{24,8},{28,20},{1,17},{... | collective-permute-start | bytes 393224 | tf_op jit(solution)/shard_map/ppermute | solution.py:383
  85.7 7.1 %collective-permute-start.20 = (bf16[128,512]{1,0:T(8,128)(2,1)S(1)}, bf16[128,512]{1,0:T(8,128)(2,1)S(1)}, u32[]{:S(2)}, u32[]{:S(2)}) collective-permute-start(bf16[128,512]{1,0:T(8,128)(2,1)S(1)} %join.6.mine_ref), channel_id=1, source_target_pairs={{0,16},{4,12},{8,24},{12,4},{16,0},{20,28},{24,8},{28,20},{1,17},{... | collective-permute-start | bytes 393224 | tf_op jit(solution)/shard_map/ppermute | solution.py:383
  90.0 6.4 %collective-permute-start.30 = (bf16[256,512]{1,0:T(8,128)(2,1)S(1)}, bf16[256,512]{1,0:T(8,128)(2,1)S(1)}, u32[]{:S(2)}, u32[]{:S(2)}) collective-permute-start(bf16[256,512]{1,0:T(8,128)(2,1)S(1)} %join.10.mine_ref), channel_id=1, source_target_pairs={{0,8},{4,20},{8,0},{12,28},{16,24},{20,4},{24,16},{28,12},{1,9},{5... | collective-permute-start | bytes 786440 | tf_op jit(solution)/shard_map/ppermute | solution.py:383
  92.9 6.4 %collective-permute-start.21 = (bf16[256,512]{1,0:T(8,128)(2,1)S(1)}, bf16[256,512]{1,0:T(8,128)(2,1)S(1)}, u32[]{:S(2)}, u32[]{:S(2)}) collective-permute-start(bf16[256,512]{1,0:T(8,128)(2,1)S(1)} %join.7.mine_ref), channel_id=1, source_target_pairs={{0,8},{4,20},{8,0},{12,28},{16,24},{20,4},{24,16},{28,12},{1,9},{5... | collective-permute-start | bytes 786440 | tf_op jit(solution)/shard_map/ppermute | solution.py:383
  96.6 11.3 %collective-permute-start.31 = (bf16[512,512]{1,0:T(8,128)(2,1)S(1)}, bf16[512,512]{1,0:T(8,128)(2,1)S(1)}, u32[]{:S(2)}, u32[]{:S(2)}) collective-permute-start(bf16[512,512]{1,0:T(8,128)(2,1)S(1)} %join.11.refs_2_), channel_id=1, source_target_pairs={{0,4},{4,0},{8,12},{12,8},{16,20},{20,16},{24,28},{28,24},{1,5},{5... | collective-permute-start | bytes 1572872 | tf_op jit(solution)/shard_map/ppermute | solution.py:383
  99.4 8.5 %collective-permute-start.22 = (bf16[512,512]{1,0:T(8,128)(2,1)S(1)}, bf16[512,512]{1,0:T(8,128)(2,1)S(1)}, u32[]{:S(2)}, u32[]{:S(2)}) collective-permute-start(bf16[512,512]{1,0:T(8,128)(2,1)S(1)} %join.8.refs_0_), channel_id=1, source_target_pairs={{0,4},{4,0},{8,12},{12,8},{16,20},{20,16},{24,28},{28,24},{1,5},{5... | collective-permute-start | bytes 1572872 | tf_op jit(solution)/shard_map/ppermute | solution.py:383

commit v3 on v2

--- a/solution.py
+++ b/solution.py
@@ -8,6 +8,7 @@
 from jax.experimental.pallas import tpu as pltpu
 from jax.sharding import PartitionSpec as P
 
+
 EDGES = 512
 ROUNDS = 2
 
@@ -17,6 +18,15 @@
 DIGIT = 3
 RADIX_BITS = 7
 PAD = 16
+
+
+def ORDERS(over_d, back_d, over_g):
+    return [(over_d + over_g, back_d + over_g), (over_g + over_d, over_g + back_d)]
+
+
+SHARES = (3, 1)
+
+
 NT = (((1,), (1,)), ((), ()))
 NN = (((1,), (0,)), ((), ()))
 BF = jnp.bfloat16
@@ -32,17 +42,59 @@
     return math.prod(shape) * jnp.dtype(dtype).itemsize
 
 
-def call(kernel, outs, args, flops=0, name=None, room=0):
-    moved = sum(size_of(a.shape, a.dtype) for a in args) + sum(size_of(*o) for o in outs)
+class Fetched:
+    def __init__(self, source, target, sems, first):
+        self.target, self.shape = target, target.shape
+        self.split = len(target.shape) == 3
+        at = range(target.shape[0]) if self.split else [...]
+        self.copies = [
+            pltpu.make_async_copy(source.at[k], target.at[k], sems.at[first + n])
+            for n, k in enumerate(at)
+        ]
+        for copy in self.copies:
+            copy.start()
+
+    def __getitem__(self, k):
+        n = k if self.split else 0
+        if self.copies[n] is not None:
+            self.copies[n].wait()
+            self.copies[n] = None
+        return self.target[k]
+
+
+def copies_of(shape):
+    return shape[0] if len(shape) == 3 else 1
+
+
+def call(kernel, outs, args, flops=0, room=0, fetch=()):
+    arrays = [*args, *fetch]
+    moved = sum(size_of(a.shape, a.dtype) for a in arrays) + sum(size_of(*o) for o in outs)
+
+    def whole(*refs):
+        first, rest = refs[: len(args)], refs[len(args) :]
+        sources, rest = rest[: len(fetch)], rest[len(fetch) :]
+        out_refs, rest = rest[: len(outs)], rest[len(outs) :]
+        copies, used = [], 0
+        for n, source in enumerate(sources):
+            copies.append(Fetched(source, rest[n], rest[-1], used))
+            used += copies_of(source.shape)
+        kernel(*first, *copies, *out_refs)
+
+    scratch = [pltpu.VMEM(a.shape, a.dtype) for a in fetch]
+    if fetch:
+        scratch.append(pltpu.SemaphoreType.DMA((sum(copies_of(a.shape) for a in fetch),)))
     return pl.pallas_call(
-        kernel,
+        whole,
         out_shape=[jax.ShapeDtypeStruct(s, d) for s, d in outs],
-        in_specs=[pl.BlockSpec(memory_space=pltpu.VMEM)] * len(args),
+        in_specs=[pl.BlockSpec(memory_space=pltpu.VMEM)] * len(args)
+        + [pl.BlockSpec(memory_space=pltpu.HBM)] * len(fetch),
         out_specs=[pl.BlockSpec(memory_space=pltpu.VMEM)] * len(outs),
-        compiler_params=pltpu.CompilerParams(vmem_limit_bytes=moved + (1 << 20) + room),
+        scratch_shapes=scratch,
+        compiler_params=pltpu.CompilerParams(
+            vmem_limit_bytes=None if room is None else moved + (1 << 20) + room
+        ),
         cost_estimate=pl.CostEstimate(flops=flops, bytes_accessed=moved, transcendentals=0),
-        name=name,
-    )(*args)
+    )(*arrays)
 
 
 def put_rows(shape, rows):
@@ -107,27 +159,34 @@
     return loss, mm(deltas, pair_b).astype(BF)
 
 
-def pair_edges(own_b, pair_b, tail, rel_ref):
-    src_row, dst_row, rel_row = decoded(tail)
+def pair_queries(pair_b, tail, rel_ref):
+    src_row, _, rel_row = decoded(tail)
     src_col, rel_col = columns([src_row, rel_row])
-    rows = own_b.shape[0]
-    src_b = mm(hit_cols(src_col, rows).astype(BF), pair_b).astype(BF)
-    queries = project(src_b, rel_col, rel_ref)
+    src_b = mm(hit_cols(src_col, pair_b.shape[0]).astype(BF), pair_b).astype(BF)
+    return project(src_b, rel_col, rel_ref)
+
+
+def pair_block(own_b, queries, tail):
+    _, dst_row, _ = decoded(tail)
     scores = mm(own_b, queries, NT)
     top = jnp.max(scores, axis=0, keepdims=True)
     exp_scores = jnp.exp(scores - top)
     total = jnp.sum(exp_scores, axis=0, keepdims=True)
-    target = hit_rows(dst_row, rows).astype(F32)
+    target = hit_rows(dst_row, own_b.shape[0]).astype(F32)
     deltas = (exp_scores / total - target).astype(BF)
-    return mm(deltas, queries).astype(BF).astype(F32)
-
-
-def row_gradient(dquery, src_row, rel_col, rel_ref, rows):
+    return mm(deltas, queries).astype(BF)
+
+
+def back_project(dquery, rel_col, rel_ref):
     total = None
     for k in range(rel_ref.shape[0]):
         part = mm(picked(dquery, rel_col, k), rel_ref[k], NT)
         total = part if total is None else total + part
-    return mm(hit_rows(src_row, rows).astype(BF), total.astype(BF))
+    return total.astype(BF)
+
+
+def add_rows(back, src_row, rows):
+    return mm(hit_rows(src_row, rows).astype(BF), back)
 
 
 def update(emb_ref, state_ref, gradient, new_ref, new_state_ref):
@@ -146,10 +205,11 @@
     return [ref[round_no : round_no + 1, :].astype(F32) for ref in refs]
 
 
-def pack_kernel(emb_ref, src_ref, dst_ref, rid_ref, out_ref):
-    rows, width = emb_ref.shape
-    out_ref[0:rows, :] = emb_ref[...].astype(BF)
-    out_ref[rows : rows + PAD, :] = encoded((src_ref, dst_ref, rid_ref), 0, width)
+def pack_kernel(emb, src, dst, rid, out_ref):
+    width = out_ref.shape[1]
+    rows = out_ref.shape[0] - PAD
+    out_ref[rows : rows + PAD, :] = encoded([x[...] for x in (src, dst, rid)], 0, width)
+    out_ref[0:rows, :] = emb[...].astype(BF)
 
 
 def project_loop(src_b, rel_col, rel_ref):
@@ -173,22 +233,41 @@
     query_body(own_ref[0:rows, :], src_ref, rid_ref, 0, rel_ref, query_ref, src_t_ref)
 
 
-def relation_part(src_t_ref, dquery, rel_col, k):
-    return mm(src_t_ref[...], picked(dquery, rel_col, k))
+def half_rows(ref, which):
+    half = ref.shape[0] // 2
+    return ref[pl.ds(pl.multiple_of(which * half, half), half), :]
+
+
+def relation_part(src_half, dquery, rel_col, k):
+    return mm(src_half, picked(dquery, rel_col, k))
 
 
 def next_query_kernel(
-    round_no, own_ref, rel_ref, src_ref, rid_ref, old_t_ref, dquery_ref, query_ref, src_t_ref, part_ref
+    round_no,
+    stage,
+    own_ref,
+    rel_ref,
+    src_ref,
+    rid_ref,
+    old_t_ref,
+    dquery_ref,
+    query_ref,
+    src_t_ref,
+    give_ref,
+    keep_ref,
 ):
     rows = own_ref.shape[0] - PAD
     query_body(own_ref[0:rows, :], src_ref, rid_ref, round_no, rel_ref, query_ref, src_t_ref)
     (rel_col,) = columns(index_rows((rid_ref,), round_no - 1))
-
-    def step(k, carry):
-        part_ref[k] = relation_part(old_t_ref, dquery_ref[...], rel_col, k.astype(F32))
-        return carry
-
-    lax.fori_loop(0, rel_ref.shape[0], step, 0)
+    upper = stage.upper()
+    for ref, which in ((give_ref, 1 - upper), (keep_ref, upper)):
+        src_half = half_rows(old_t_ref, which)
+
+        def step(k, carry, ref=ref, src_half=src_half):
+            ref[k] = relation_part(src_half, dquery_ref[...], rel_col, k.astype(F32))
+            return carry
+
+        lax.fori_loop(0, ref.shape[0], step, 0)
 
 
 def round_kernel(
@@ -198,10 +277,10 @@
     emb_ref,
     state_ref,
     query_ref,
-    rel_ref,
     src_ref,
     dst_ref,
     rid_ref,
+    rel_ref,
     new_ref,
     next_ref,
     new_state_ref,
@@ -215,8 +294,10 @@
     loss, dquery = own_edges(query_ref[...], pair_b, dst_col)
     loss_ref[...] = jnp.broadcast_to(loss, loss_ref.shape)
     dquery_ref[...] = dquery
-    gradient = pair_edges(own_ref[0:rows, :], pair_b, pair_ref[rows : rows + PAD, :], rel_ref)
-    gradient = gradient + row_gradient(dquery, src_row, rel_col, rel_ref, rows)
+    tail = pair_ref[rows : rows + PAD, :]
+    block = pair_block(own_ref[0:rows, :], pair_queries(pair_b, tail, rel_ref), tail)
+    back = back_project(dquery, rel_col, rel_ref)
+    gradient = block.astype(F32) + add_rows(back, src_row, rows)
     new_rows = update(emb_ref, state_ref, gradient, new_ref, new_state_ref)
     next_ref[0:rows, :] = new_rows.astype(BF)
     next_ref[rows : rows + PAD, :] = encoded((src_ref, dst_ref, rid_ref), round_no + 1, width)
@@ -230,8 +311,8 @@
     src_t_ref,
     dst_ref,
     rid_ref,
-    part_ref,
     old_loss_ref,
+    old,
     dquery_ref,
     loss_ref,
     *give_refs,
@@ -242,48 +323,53 @@
     dquery_ref[...] = dquery
     total = old_loss_ref[...] + loss
     loss_ref[...] = total
-    upper = stage.upper()
+    src_half = half_rows(src_t_ref, 1 - stage.upper())
+    at = 0
     for n, give_ref in enumerate(give_refs):
-        k = 2 * n + 1 - upper
-        if n == 0:
+        base = 0
+        if n == len(give_refs) - 1:
             give_ref[0:PAD, :] = loss_tail(total)
             base = PAD
-        else:
-            base = 0
-        part = relation_part(src_t_ref, dquery, rel_col, k.astype(F32)) + part_ref[k]
-        give_ref[base : base + part.shape[0], :] = part.astype(BF)
+        half = src_half.shape[0]
+        for j in range((give_ref.shape[0] - base) // half):
+            part = relation_part(src_half, dquery, rel_col, at) + old[at]
+            give_ref[base + j * half : base + (j + 1) * half, :] = part.astype(BF)
+            at += 1
 
 
 def keep_kernel(round_no, stage, src_t_ref, dquery_ref, rid_ref, part_ref, *keep_refs):
     (rel_col,) = columns(index_rows((rid_ref,), round_no))
-    upper = stage.upper()
-    for n, keep_ref in enumerate(keep_refs):
-        k = 2 * n + upper
-        keep_ref[...] = (
-            relation_part(src_t_ref, dquery_ref[...], rel_col, k.astype(F32)) + part_ref[k]
-        )
+    src_half = half_rows(src_t_ref, stage.upper())
+    half = src_half.shape[0]
+    at = 0
+    for keep_ref in keep_refs:
+        for j in range(keep_ref.shape[0] // half):
+            part = relation_part(src_half, dquery_ref[...], rel_col, at) + part_ref[at]
+            keep_ref[j * half : (j + 1) * half, :] = part
+            at += 1
+
+
+def pair_query_kernel(pair_ref, rel_ref, query_ref):
+    rows = pair_ref.shape[0] - PAD
+    query_ref[...] = pair_queries(pair_ref[0:rows, :], pair_ref[rows : rows + PAD, :], rel_ref)
+
+
+def pair_block_kernel(pair_ref, own_ref, query_ref, block_ref):
+    rows = own_ref.shape[0] - PAD
+    tail = pair_ref[rows : rows + PAD, :]
+    block_ref[...] = pair_block(own_ref[0:rows, :], query_ref[...], tail)
+
+
+def back_kernel(round_no, dquery_ref, rid_ref, rel_ref, back_ref):
+    (rel_col,) = columns(index_rows((rid_ref,), round_no))
+    back_ref[...] = back_project(dquery_ref[...], rel_col, rel_ref)
 
 
 def last_rows_kernel(
-    round_no,
-    pair_ref,
-    own_ref,
-    emb_ref,
-    state_ref,
-    dquery_ref,
-    rel_ref,
-    src_ref,
-    rid_ref,
-    new_ref,
-    new_state_ref,
+    round_no, emb_ref, state_ref, block_ref, back_ref, src_ref, new_ref, new_state_ref
 ):
-    rows = emb_ref.shape[0]
-    src_row, rel_row = index_rows((src_ref, rid_ref), round_no)
-    (rel_col,) = columns([rel_row])
-    gradient = pair_edges(
-        own_ref[0:rows, :], pair_ref[0:rows, :], pair_ref[rows : rows + PAD, :], rel_ref
-    )
-    gradient = gradient + row_gradient(dquery_ref[...], src_row, rel_col, rel_ref, rows)
+    (src_row,) = index_rows((src_ref,), round_no)
+    gradient = block_ref[...].astype(F32) + add_rows(back_ref[...], src_row, emb_ref.shape[0])
     update(emb_ref, state_ref, gradient, new_ref, new_state_ref)
 
 
@@ -344,53 +430,47 @@
     out_ref[half : 2 * half, :] = jnp.where(upper, mine, came)
 
 
-def spread_kernel(stage, *refs):
-    out_ref = refs[-1]
-    k = pl.program_id(0)
-    upper = stage.upper()
-    for n in range(len(refs) // 2):
-        mine_ref, came_ref = refs[2 * n], refs[2 * n + 1]
-
-        @pl.when(k == 2 * n + upper)
-        def _(mine_ref=mine_ref):
-            out_ref[0] = mine_ref[...].astype(F32)
-
-        @pl.when(k == 2 * n + 1 - upper)
-        def _(came_ref=came_ref):
-            out_ref[0] = came_ref[...].astype(F32)
-
-
 def xor_route(axis, mask):
     return [(low, low ^ mask) for low in range(lax.axis_size(axis))]
 
 
 class Stage:
-    def __init__(self, axis, even_bit, odd_bit):
-        self.axis, self.even_bit, self.odd_bit = axis, even_bit, odd_bit
-        self.route = [
-            (n, n ^ (1 << (odd_bit if n & 1 else even_bit))) for n in range(lax.axis_size(axis))
-        ]
+    def __init__(self, even, odd):
+        self.even, self.odd = even, odd
+        count_d, count_g = lax.axis_size("dom"), lax.axis_size("grp")
+        self.route = []
+        for me_d in range(count_d):
+            for me_g in range(count_g):
+                axis, bit = odd if me_d & 1 else even
+                to_d = me_d ^ (1 << bit if axis == "dom" else 0)
+                to_g = me_g ^ (1 << bit if axis == "grp" else 0)
+                self.route.append((me_d * count_g + me_g, to_d * count_g + to_g))
 
     def upper(self):
-        me = lax.axis_index(self.axis)
-        even = jnp.bitwise_and(jnp.right_shift(me, self.even_bit), 1)
-        if self.even_bit == self.odd_bit:
-            return even
-        odd = jnp.bitwise_and(jnp.right_shift(me, self.odd_bit), 1)
-        return jnp.where(jnp.bitwise_and(me, 1) == 1, odd, even)
+        def read(axis, bit):
+            return jnp.bitwise_and(jnp.right_shift(lax.axis_index(axis), bit), 1)
+
+        if self.even == self.odd:
+            return read(*self.even)
+        return jnp.where(read("dom", 0) == 1, read(*self.odd), read(*self.even))
 
     def swap(self, block):
-        return lax.ppermute(block, self.axis, self.route)
-
-
-def make_stages():
-    bits_d = lax.axis_size("dom").bit_length() - 1
-    bits_g = lax.axis_size("grp").bit_length() - 1
-    up = list(range(1, bits_d))
-    stages = [Stage("dom", 0, 0)]
-    stages += [Stage("dom", a, b) for a, b in zip(up, up[::-1])]
-    stages += [Stage("grp", bit, bit) for bit in range(bits_g)]
-    return stages
+        return lax.ppermute(block, ("dom", "grp"), self.route)
+
+
+def bit_lists(bits_d, bits_g):
+    return [("dom", bit) for bit in range(1, bits_d)], [("grp", bit) for bit in range(bits_g)]
+
+
+def make_orders():
+    over_d, over_g = bit_lists(
+        lax.axis_size("dom").bit_length() - 1, lax.axis_size("grp").bit_length() - 1
+    )
+    back_d = over_d[::-1]
+    orders = []
+    for even, odd in ORDERS(over_d, back_d, over_g):
+        orders.append([Stage(("dom", 0), ("dom", 0))] + [Stage(*pair) for pair in zip(even, odd)])
+    return orders
 
 
 def halve(stage, came, keep, loss, final):
@@ -418,9 +498,7 @@
     if with_loss:
         outs.append((loss.shape, F32))
         args.append(loss)
-    got = list(
-        call(functools.partial(halve_kernel, with_loss, final, stage), outs, args, name="halve")
-    )
+    got = list(call(functools.partial(halve_kernel, with_loss, final, stage), outs, args))
     give = got.pop(0)
     rest = None if final else got.pop(0)
     return give, rest, (got.pop(0) if with_loss else None)
@@ -437,7 +515,7 @@
     if with_loss:
         outs.append((loss.shape, F32))
         args.append(loss)
-    got = call(functools.partial(meet_kernel, with_loss), outs, args, name="meet")
+    got = call(functools.partial(meet_kernel, with_loss), outs, args)
     return got[0], (got[1] if with_loss else None)
 
 
@@ -446,46 +524,74 @@
     if half % ROW_BLOCK:
         upper = stage.upper() == 1
         return jnp.concatenate([jnp.where(upper, came, mine), jnp.where(upper, mine, came)])
-    (out,) = call(
-        functools.partial(join_kernel, stage), [((2 * half, width), BF)], [mine, came], name="join"
-    )
+    (out,) = call(functools.partial(join_kernel, stage), [((2 * half, width), BF)], [mine, came])
     return out
 
 
-def all_sum(stages, gives, keeps, loss):
-    losses = [loss] + [None] * (len(gives) - 1)
+def all_sum(orders, gives, keeps, loss, shape):
+    streams = range(len(gives))
+    losses = [None] * (len(gives) - 1) + [loss]
     gives, keeps = list(gives), list(keeps)
-    streams = range(len(gives))
-    for at, stage in enumerate(stages[:-1]):
-        final = at == len(stages) - 2
+    count = len(orders[0])
+    for at in range(count - 1):
         for n in streams:
-            came = stage.swap(gives[n])
+            came = orders[n][at].swap(gives[n])
             gives[n], keeps[n], losses[n] = halve(
-                stages[at + 1], came, keeps[n], losses[n], final
+                orders[n][at + 1], came, keeps[n], losses[n], at == count - 2
             )
     values = [None] * len(gives)
     for n in streams:
-        came = stages[-1].swap(gives[n])
+        came = orders[n][-1].swap(gives[n])
         values[n], losses[n] = meet(came, gives[n], losses[n])
-    for stage in stages[-2:0:-1]:
+    for at in range(count - 2, 0, -1):
         for n in streams:
-            came = stage.swap(values[n])
-            values[n] = join(stage, values[n], came)
-    pairs = []
+            came = orders[n][at].swap(values[n])
+            values[n] = join(orders[n][at], values[n], came)
+    came = []
     for n in streams:
-        pairs += [values[n], stages[0].swap(values[n])]
-    rows, width = values[0].shape
-    count = 2 * len(gives)
-    total = pl.pallas_call(
-        functools.partial(spread_kernel, stages[0]),
-        grid=(count,),
-        out_shape=jax.ShapeDtypeStruct((count, rows, width), F32),
-        in_specs=[pl.BlockSpec(memory_space=pltpu.VMEM)] * count,
-        out_specs=pl.BlockSpec((1, rows, width), lambda k: (k, 0, 0)),
+        came.append(orders[n][0].swap(values[n]))
+    core = orders[0][0]
+    total = spread(core, shape, values, None)
+    total = spread(core, shape, came, total)
+    return total, losses[-1][0, 0]
+
+
+def spread_kernel(stage, flip, streams, *refs):
+    value_refs, (out_ref, wide_ref, sems) = refs[:streams], refs[-3:]
+    half = out_ref.shape[1] // 2
+    which = 1 - stage.upper() if flip else stage.upper()
+    rows = pl.ds(pl.multiple_of(which * half, half), half)
+    at, copies = 0, []
+    for value_ref in value_refs:
+        for j in range(value_ref.shape[0] // half):
+            wide_ref[at] = value_ref[j * half : (j + 1) * half, :].astype(F32)
+            copies.append(
+                pltpu.make_async_copy(wide_ref.at[at], out_ref.at[at, rows, :], sems.at[at])
+            )
+            copies[-1].start()
+            at += 1
+    for copy in copies:
+        copy.wait()
+
+
+def spread(stage, shape, values, total):
+    known = [] if total is None else [total]
+    count, rows, width = shape
+    return pl.pallas_call(
+        functools.partial(spread_kernel, stage, bool(known), len(values)),
+        out_shape=jax.ShapeDtypeStruct(shape, F32),
+        in_specs=[pl.BlockSpec(memory_space=pltpu.VMEM)] * len(values)
+        + [pl.BlockSpec(memory_space=pltpu.HBM)] * len(known),
+        out_specs=pl.BlockSpec(memory_space=pltpu.HBM),
+        scratch_shapes=[
+            pltpu.VMEM((count, rows // 2, width), F32),
+            pltpu.SemaphoreType.DMA((count,)),
+        ],
+        input_output_aliases={len(values): 0} if known else {},
         compiler_params=pltpu.CompilerParams(vmem_limit_bytes=8 << 20),
+        cost_estimate=pl.CostEstimate(flops=0, bytes_accessed=4 << 20, transcendentals=0),
         name="spread",
-    )(*pairs)
-    return total, losses[0][0, 0]
+    )(*values, *known)
 
 
 def exchange(block, axis, mask, beside):
@@ -521,14 +627,16 @@
     emb = embeddings[0]
     src, dst, rid = src_rows[0, 0], dst_rows[0, 0], rel_ids[0, 0]
     square = 2 * rows * width * edges
-    stages = make_stages()
+    orders = make_orders()
     packed = ((rows + PAD, width), BF)
     edge_b = ((edges, width), BF)
     edge_t = ((width, edges), BF)
-    part = (relations.shape, F32)
+    half = width // 2
+    part = ((count, half, width), F32)
+    sizes = [count * share // 4 for share in SHARES]
     line = ((8, width), F32)
 
-    (own,) = call(pack_kernel, [packed], [emb, src, dst, rid], name="pack")
+    (own,) = call(pack_kernel, [packed], [], room=None, fetch=[emb, src, dst, rid])
     pair, (rel_b, query, src_t) = exchange(
         own,
         "dom",
@@ -539,7 +647,6 @@
                 [(relations.shape, BF), edge_b, edge_t],
                 [own, relations, src, rid],
                 flops=5 * square,
-                name="query",
                 room=6 << 20,
             )
         ),
@@ -547,52 +654,70 @@
     new, own_next, state, dquery, loss = call(
         functools.partial(round_kernel, 0),
         [((rows, width), F32), packed, ((1, rows), F32), edge_b, line],
-        [pair, own, emb, ada_state, query, rel_b, src, dst, rid],
+        [pair, own, emb, ada_state, query, src, dst, rid],
+        fetch=[rel_b],
         flops=14 * square,
-        name="round",
         room=12 << 20,
     )
-    pair, (query, src_t, rel_part) = exchange(
+    pair, (query, src_t, give_part, keep_part) = exchange(
         own_next,
         "dom",
         plan[1],
         lambda: tuple(
             call(
-                functools.partial(next_query_kernel, 1),
-                [edge_b, edge_t, part],
+                functools.partial(next_query_kernel, 1, orders[0][0]),
+                [edge_b, edge_t, part, part],
                 [own_next, rel_b, src, rid, src_t, dquery],
                 flops=9 * square,
-                name="query",
                 room=6 << 20,
             )
         ),
     )
-    halves = count // 2
     dquery, loss, *gives = call(
-        functools.partial(last_own_kernel, 1, stages[0]),
-        [edge_b, line] + [((PAD + width, width), BF)] + [((width, width), BF)] * (halves - 1),
-        [pair, query, src_t, dst, rid, rel_part, loss],
+        functools.partial(last_own_kernel, 1, orders[0][0]),
+        [edge_b, line]
+        + [
+            ((size * half + (PAD if n == len(sizes) - 1 else 0), width), BF)
+            for n, size in enumerate(sizes)
+        ],
+        [pair, query, src_t, dst, rid, loss],
+        fetch=[give_part],
         flops=4 * square,
-        name="own",
         room=8 << 20,
     )
     keeps = call(
-        functools.partial(keep_kernel, 1, stages[0]),
-        [((width, width), F32)] * halves,
-        [src_t, dquery, rid, rel_part],
+        functools.partial(keep_kernel, 1, orders[0][0]),
+        [((size * half, width), F32) for size in sizes],
+        [src_t, dquery, rid, keep_part],
         flops=2 * square,
-        name="keep",
         room=4 << 20,
+    )
+    (pair_query,) = call(
+        pair_query_kernel, [edge_b], [pair], flops=5 * square, room=6 << 20, fetch=[rel_b]
+    )
+    (back,) = call(
+        functools.partial(back_kernel, 1),
+        [edge_b],
+        [dquery, rid],
+        flops=4 * square,
+        room=4 << 20,
+        fetch=[rel_b],
+    )
+    (block,) = call(
+        pair_block_kernel,
+        [((rows, width), BF)],
+        [pair, own_next, pair_query],
+        flops=3 * square,
+        room=6 << 20,
     )
     new, state = call(
         functools.partial(last_rows_kernel, 1),
         [((rows, width), F32), ((1, rows), F32)],
-        [pair, own_next, new, state, dquery, rel_b, src, rid],
-        flops=12 * square,
-        name="rows",
-        room=10 << 20,
-    )
-    rel_total, loss_total = all_sum(stages, gives, keeps, loss)
+        [new, state, block, back, src],
+        flops=2 * square,
+        room=6 << 20,
+    )
+    rel_total, loss_total = all_sum(orders, gives, keeps, loss, relations.shape)
     mean_loss = loss_total / (lax.axis_size("dom") * lax.axis_size("grp") * ROUNDS * EDGES)
     return (new[None], state, rel_total, mean_loss)
 

time: 111 us -> 143 us (1.29)
  waiting for transfers between devices: 33.1 us -> 60.9 us
  Pallas kernels: 40.3 us -> 43.2 us
  starting transfers between devices: 30.2 us -> 32.9 us
  local copies, waits for them, and re-layouts: 3.78 us -> 1.86 us
    ppermute x18, waiting for transfers between devices: 22.7 us -> 50.5 us  [swap(): return lax.ppermute(block, ('dom', 'grp'), self.route)]
    ppermute x18, starting transfers between devices: 23.3 us -> 27.1 us  [swap(): return lax.ppermute(block, ('dom', 'grp'), self.route)]
    pallas_call x24 -> x28, Pallas kernels: 40.3 us -> 43.2 us  [the longest x26 40.4 us: call(): pl.pallas_call(whole, out_shape=[jax.ShapeDtypeStruct(s, d) for s, d in o...]
    unnamed x22 -> x12, local copies, waits for them, and re-layouts: 1.96 us -> 0.04 us
  transfers between devices with their start and end apart: 20 -> 20, of which waited for: 14 -> 16; matrix products, arithmetic and copies ran while one was open for 0% -> 0% of each run, Pallas kernels for 22% -> 20%
where the time goes in v3:
time: 143 us
  waiting for transfers between devices  60.9 us (43%)
  Pallas kernels  43.2 us (30%)
  starting transfers between devices  32.9 us (23%)
  between operations  3.98 us (3%)
  local copies, waits for them, and re-layouts  1.86 us (1%)
    ppermute x18, waiting for transfers between devices, swap(): return lax.ppermute(block, ('dom', 'grp'), self.route)  50.5 us
    pallas_call x26, Pallas kernels, call(): pl.pallas_call(whole, out_shape=[jax.ShapeDtypeStruct(s, d) for s, d in o...  40.4 us
    ppermute x18, starting transfers between devices, swap(): return lax.ppermute(block, ('dom', 'grp'), self.route)  27.1 us
    ppermute x2, waiting for transfers between devices, branch(): x = lax.ppermute(x, axis, xor_route(axis, value << done))  10.4 us
    ppermute x2, starting transfers between devices, branch(): x = lax.ppermute(x, axis, xor_route(axis, value << done))  5.78 us
  transfers between devices with their start and end apart: 20, of which 16 were waited for; matrix products, arithmetic and copies ran while one was open for 0% of the time, Pallas kernels for 20%

profile of v3, /device:TPU:0, one launch (start us, length us, event | category | flops | bytes accessed | tf_op | source)
XLA Modules:
  0.0 142.9 jit_solution(9860739915945983523)
XLA Ops:
  0.6 1.3 fusion
  3.2 1.3 shard_map.102.refs_1_
  4.6 0.0 copy-start
  4.6 0.0 copy-start.1
  4.6 0.0 copy-start.2
  4.6 15.2 %conditional.2 = (bf16[528,512]{1,0:T(8,128)(2,1)}, bf16[4,512,512]{2,1,0:T(8,128)(2,1)}, bf16[512,512]{1,0:T(8,128)(2,1)}, bf16[512,512]{1,0:T(8,128)(2,1)}) conditional(s32[]{:T(128)} %bitcast, (bf16[528,512]{1,0:T(8,128)(2,1)S(1)}, f32[4,512,512]{2,1,0:T(8,128)}, s32[2,512]{1,0:T(2,128)}, ...), branch_computations={%region_0.0_spmd, %region_1.0_spmd, %region_2.0_spmd, %region_3.0_... | conditional | flops 1342177280 | bytes 10051656 | solution.py:617
  4.6 2.5 %collective-permute-start.2 = (bf16[528,512]{1,0:T(8,128)(2,1)S(1)}, bf16[528,512]{1,0:T(8,128)(2,1)}, u32[]{:S(2)}, u32[]{:S(2)}) collective-permute-start(bf16[528,512]{1,0:T(8,128)(2,1)S(1)} %get-tuple-element.154.refs_0_), channel_id=1, source_target_pairs={{0,12},{4,8},{8,4},{12,0},{16,28},{20,24},{24,20},{28,16},{1,13},{... | collective-permute-start | bytes 1622024 | tf_op jit(solution)/shard_map/cond/branch_2_fun/ppermute | solution.py:610
  7.1 6.6 %branch_2_fun.2 = (bf16[4,512,512]{2,1,0:T(8,128)(2,1)}, bf16[512,512]{1,0:T(8,128)(2,1)}, bf16[512,512]{1,0:T(8,128)(2,1)}) custom-call(bf16[528,512]{1,0:T(8,128)(2,1)S(1)} %get-tuple-element.154.refs_0_, f32[4,512,512]{2,1,0:T(8,128)} %get-tuple-element.155.refs_1_, s32[2,512]{1,0:T(2,128)} %get-tuple-element.156.refs_2_, s32[2,512]{1,0:T(2,128)} %get-tuple-element.157.refs_3_), custom_call_target="tpu_custom_call" | custom-call | flops 1342177280 | bytes 7888896 | tf_op jit(solution)/shard_map/cond/branch_2_fun/pallas_call | solution.py:86
  13.7 6.0 %collective-permute-done.2 = bf16[528,512]{1,0:T(8,128)(2,1)} collective-permute-done((bf16[528,512]{1,0:T(8,128)(2,1)S(1)}, bf16[528,512]{1,0:T(8,128)(2,1)}, u32[]{:S(2)}, u32[]{:S(2)}) %collective-permute-start.2) | collective-permute-done | bytes 540704 | tf_op jit(solution)/shard_map/cond/branch_2_fun/ppermute | solution.py:610
  19.8 0.0 copy-start.3
  19.8 0.0 copy-start.4
  19.8 8.5 %shard_map.103 = (f32[512,512]{1,0:T(8,128)S(1)}, bf16[528,512]{1,0:T(8,128)(2,1)S(1)}, f32[1,512]{1,0:T(1,128)S(1)}, bf16[512,512]{1,0:T(8,128)(2,1)S(1)}, f32[8,512]{1,0:T(8,128)S(1)}) custom-call(bf16[528,512]{1,0:T(8,128)(2,1)} %get-tuple-element.304.refs_0_, bf16[528,512]{1,0:T(8,128)(2,1)S(1)} %shard_map.102.refs_1_, f32[512,512]{1,0:T(8,128)S(1)} %bitcast.9, ...), custom_call_target="tpu_custom_call" | custom-call | flops 3758096384 | bytes 6897664 | tf_op jit(solution)/shard_map/pallas_call | solution.py:86
  28.4 15.7 %conditional.3 = (bf16[528,512]{1,0:T(8,128)(2,1)}, bf16[512,512]{1,0:T(8,128)(2,1)S(1)}, bf16[512,512]{1,0:T(8,128)(2,1)S(1)}, f32[4,256,512]{2,1,0:T(8,128)S(1)}, f32[4,256,512]{2,1,0:T(8,128)S(1)}) conditional(s32[]{:T(128)} %bitcast.5, (bf16[528,512]{1,0:T(8,128)(2,1)S(1)}, bf16[4,512,512]{2,1,0:T(8,128)(2,1)}, ...), branch_computations={%region_7.0_spmd, %region_8.0_spmd, %region_9.0_spmd, %region_10.0... | conditional | flops 2415919104 | bytes 11100240 | solution.py:617
  28.4 3.3 %collective-permute-start.13 = (bf16[528,512]{1,0:T(8,128)(2,1)S(1)}, bf16[528,512]{1,0:T(8,128)(2,1)}, u32[]{:S(2)}, u32[]{:S(2)}) collective-permute-start(bf16[528,512]{1,0:T(8,128)(2,1)S(1)} %get-tuple-element.249.refs_0_), channel_id=1, source_target_pairs={{0,28},{4,24},{8,20},{12,16},{16,12},{20,8},{24,4},{28,0},{1,29},{... | collective-permute-start | bytes 1622024 | tf_op jit(solution)/shard_map/cond/branch_6_fun/ppermute | solution.py:610
  31.7 8.0 %branch_6_fun.3 = (bf16[512,512]{1,0:T(8,128)(2,1)S(1)}, bf16[512,512]{1,0:T(8,128)(2,1)S(1)}, f32[4,256,512]{2,1,0:T(8,128)S(1)}, f32[4,256,512]{2,1,0:T(8,128)S(1)}) custom-call(bf16[528,512]{1,0:T(8,128)(2,1)S(1)} %get-tuple-element.249.refs_0_, bf16[4,512,512]{2,1,0:T(8,128)(2,1)} %get-tuple-element.250.refs_1_, ...), custom_call_target="tpu_custom_call" | custom-call | flops 2415919104 | bytes 8937472 | tf_op jit(solution)/shard_map/cond/branch_6_fun/pallas_call | solution.py:86
  39.7 4.4 %collective-permute-done.13 = bf16[528,512]{1,0:T(8,128)(2,1)} collective-permute-done((bf16[528,512]{1,0:T(8,128)(2,1)S(1)}, bf16[528,512]{1,0:T(8,128)(2,1)}, u32[]{:S(2)}, u32[]{:S(2)}) %collective-permute-start.13) | collective-permute-done | bytes 540704 | tf_op jit(solution)/shard_map/cond/branch_6_fun/ppermute | solution.py:610
  44.1 3.6 %shard_map.106 = (bf16[512,512]{1,0:T(8,128)(2,1)S(1)}, f32[8,512]{1,0:T(8,128)S(1)}, bf16[768,512]{1,0:T(8,128)(2,1)S(1)}, bf16[272,512]{1,0:T(8,128)(2,1)S(1)}) custom-call(bf16[528,512]{1,0:T(8,128)(2,1)} %get-tuple-element.312.refs_0_, bf16[512,512]{1,0:T(8,128)(2,1)S(1)} %get-tuple-element.313.refs_1_, ...), custom_call_target="tpu_custom_call" | custom-call | flops 1073741824 | bytes 5316608 | tf_op jit(solution)/shard_map/pallas_call | solution.py:86
  47.7 0.5 collective-permute-start.14
  48.2 1.1 shard_map.109
  49.3 0.8 collective-permute-done.14.refs_0_
  50.1 0.2 shard_map.110
  50.3 2.3 %collective-permute-start.15 = (bf16[384,512]{1,0:T(8,128)(2,1)S(1)}, bf16[384,512]{1,0:T(8,128)(2,1)S(1)}, u32[]{:S(2)}, u32[]{:S(2)}) collective-permute-start(bf16[384,512]{1,0:T(8,128)(2,1)S(1)} %get-tuple-element.323), channel_id=1, source_target_pairs={{0,8},{1,9},{2,10},{3,11},{4,20},{5,21},{6,22},{7,23},{8,0},{9,1},... | collective-permute-start | bytes 1179656 | tf_op jit(solution)/shard_map/ppermute | solution.py:458
  52.6 5.8 %collective-permute-done.15.refs_0_ = bf16[384,512]{1,0:T(8,128)(2,1)S(1)} collective-permute-done((bf16[384,512]{1,0:T(8,128)(2,1)S(1)}, bf16[384,512]{1,0:T(8,128)(2,1)S(1)}, u32[]{:S(2)}, u32[]{:S(2)}) %collective-permute-start.15) | collective-permute-done | bytes 393248 | tf_op jit(solution)/shard_map/ppermute | solution.py:458
  58.3 0.1 shard_map.111
  58.5 2.1 %collective-permute-start.16 = (bf16[192,512]{1,0:T(8,128)(2,1)S(1)}, bf16[192,512]{1,0:T(8,128)(2,1)S(1)}, u32[]{:S(2)}, u32[]{:S(2)}) collective-permute-start(bf16[192,512]{1,0:T(8,128)(2,1)S(1)} %get-tuple-element.325), channel_id=1, source_target_pairs={{0,16},{1,17},{2,18},{3,19},{4,12},{5,13},{6,14},{7,15},{8,24},{9,... | collective-permute-start | bytes 589832 | tf_op jit(solution)/shard_map/ppermute | solution.py:458
  60.5 3.7 %collective-permute-done.16.refs_0_ = bf16[192,512]{1,0:T(8,128)(2,1)S(1)} collective-permute-done((bf16[192,512]{1,0:T(8,128)(2,1)S(1)}, bf16[192,512]{1,0:T(8,128)(2,1)S(1)}, u32[]{:S(2)}, u32[]{:S(2)}) %collective-permute-start.16) | collective-permute-done | bytes 196640 | tf_op jit(solution)/shard_map/ppermute | solution.py:458
  64.2 2.1 %collective-permute-start.17 = (bf16[96,512]{1,0:T(8,128)(2,1)S(1)}, bf16[96,512]{1,0:T(8,128)(2,1)S(1)}, u32[]{:S(2)}, u32[]{:S(2)}) collective-permute-start(bf16[96,512]{1,0:T(8,128)(2,1)S(1)} %get-tuple-element.327), channel_id=1, source_target_pairs={{0,1},{1,0},{2,3},{3,2},{4,5},{5,4},{6,7},{7,6},{8,9},{9,8},{10,11... | collective-permute-start | bytes 294920 | tf_op jit(solution)/shard_map/ppermute | solution.py:458
  66.4 2.6 %collective-permute-done.17.refs_0_ = bf16[96,512]{1,0:T(8,128)(2,1)S(1)} collective-permute-done((bf16[96,512]{1,0:T(8,128)(2,1)S(1)}, bf16[96,512]{1,0:T(8,128)(2,1)S(1)}, u32[]{:S(2)}, u32[]{:S(2)}) %collective-permute-start.17) | collective-permute-done | bytes 98336 | tf_op jit(solution)/shard_map/ppermute | solution.py:458
  69.0 3.2 %collective-permute-start.18 = (bf16[96,512]{1,0:T(8,128)(2,1)S(1)}, bf16[96,512]{1,0:T(8,128)(2,1)S(1)}, u32[]{:S(2)}, u32[]{:S(2)}) collective-permute-start(bf16[96,512]{1,0:T(8,128)(2,1)S(1)} %shard_map.113.refs_1_), channel_id=1, source_target_pairs={{0,2},{1,3},{2,0},{3,1},{4,6},{5,7},{6,4},{7,5},{8,10},{9,11},{10,... | collective-permute-start | bytes 294920 | tf_op jit(solution)/shard_map/ppermute | solution.py:458
  72.2 3.1 %collective-permute-done.18.refs_0_ = bf16[96,512]{1,0:T(8,128)(2,1)S(1)} collective-permute-done((bf16[96,512]{1,0:T(8,128)(2,1)S(1)}, bf16[96,512]{1,0:T(8,128)(2,1)S(1)}, u32[]{:S(2)}, u32[]{:S(2)}) %collective-permute-start.18) | collective-permute-done | bytes 98336 | tf_op jit(solution)/shard_map/ppermute | solution.py:458
  75.3 1.6 %collective-permute-start.19 = (bf16[96,512]{1,0:T(8,128)(2,1)S(1)}, bf16[96,512]{1,0:T(8,128)(2,1)S(1)}, u32[]{:S(2)}, u32[]{:S(2)}) collective-permute-start(bf16[96,512]{1,0:T(8,128)(2,1)S(1)} %shard_map.114.refs_0_), channel_id=1, source_target_pairs={{0,1},{1,0},{2,3},{3,2},{4,5},{5,4},{6,7},{7,6},{8,9},{9,8},{10,11... | collective-permute-start | bytes 294920 | tf_op jit(solution)/shard_map/ppermute | solution.py:458
  76.9 3.1 %collective-permute-done.19.refs_1_ = bf16[96,512]{1,0:T(8,128)(2,1)S(1)} collective-permute-done((bf16[96,512]{1,0:T(8,128)(2,1)S(1)}, bf16[96,512]{1,0:T(8,128)(2,1)S(1)}, u32[]{:S(2)}, u32[]{:S(2)}) %collective-permute-start.19) | collective-permute-done | bytes 98336 | tf_op jit(solution)/shard_map/ppermute | solution.py:458
  80.0 1.7 %collective-permute-start.20 = (bf16[192,512]{1,0:T(8,128)(2,1)S(1)}, bf16[192,512]{1,0:T(8,128)(2,1)S(1)}, u32[]{:S(2)}, u32[]{:S(2)}) collective-permute-start(bf16[192,512]{1,0:T(8,128)(2,1)S(1)} %shard_map.115.refs_0_), channel_id=1, source_target_pairs={{0,16},{1,17},{2,18},{3,19},{4,12},{5,13},{6,14},{7,15},{8,24},{9,... | collective-permute-start | bytes 589832 | tf_op jit(solution)/shard_map/ppermute | solution.py:458
  81.8 5.3 %collective-permute-done.20.refs_1_ = bf16[192,512]{1,0:T(8,128)(2,1)S(1)} collective-permute-done((bf16[192,512]{1,0:T(8,128)(2,1)S(1)}, bf16[192,512]{1,0:T(8,128)(2,1)S(1)}, u32[]{:S(2)}, u32[]{:S(2)}) %collective-permute-start.20) | collective-permute-done | bytes 196640 | tf_op jit(solution)/shard_map/ppermute | solution.py:458
  87.1 1.6 %collective-permute-start.21 = (bf16[384,512]{1,0:T(8,128)(2,1)S(1)}, bf16[384,512]{1,0:T(8,128)(2,1)S(1)}, u32[]{:S(2)}, u32[]{:S(2)}) collective-permute-start(bf16[384,512]{1,0:T(8,128)(2,1)S(1)} %shard_map.116.refs_0_), channel_id=1, source_target_pairs={{0,8},{1,9},{2,10},{3,11},{4,20},{5,21},{6,22},{7,23},{8,0},{9,1},... | collective-permute-start | bytes 1179656 | tf_op jit(solution)/shard_map/ppermute | solution.py:458
  88.7 0.0 collective-permute-done.23.refs_0_
  88.7 0.1 shard_map.118
  88.8 1.4 collective-permute-start.24
  90.2 4.8 %collective-permute-done.21.refs_1_ = bf16[384,512]{1,0:T(8,128)(2,1)S(1)} collective-permute-done((bf16[384,512]{1,0:T(8,128)(2,1)S(1)}, bf16[384,512]{1,0:T(8,128)(2,1)S(1)}, u32[]{:S(2)}, u32[]{:S(2)}) %collective-permute-start.21) | collective-permute-done | bytes 393248 | tf_op jit(solution)/shard_map/ppermute | solution.py:458
  95.0 0.1 shard_map.117.refs_0_
  95.1 0.1 collective-permute-start.22
  95.1 0.0 collective-permute-done.24.refs_0_
  95.1 0.1 shard_map.119
  95.2 3.4 %collective-permute-start.25 = (bf16[80,512]{1,0:T(8,128)(2,1)S(1)}, bf16[80,512]{1,0:T(8,128)(2,1)S(1)}, u32[]{:S(2)}, u32[]{:S(2)}) collective-permute-start(bf16[80,512]{1,0:T(8,128)(2,1)S(1)} %get-tuple-element.335), channel_id=1, source_target_pairs={{0,2},{1,3},{2,0},{3,1},{4,6},{5,7},{6,4},{7,5},{8,10},{9,11},{10,... | collective-permute-start | bytes 245768 | tf_op jit(solution)/shard_map/ppermute | solution.py:458
  98.6 4.9 %collective-permute-done.25.refs_0_ = bf16[80,512]{1,0:T(8,128)(2,1)S(1)} collective-permute-done((bf16[80,512]{1,0:T(8,128)(2,1)S(1)}, bf16[80,512]{1,0:T(8,128)(2,1)S(1)}, u32[]{:S(2)}, u32[]{:S(2)}) %collective-permute-start.25) | collective-permute-done | bytes 81952 | tf_op jit(solution)/shard_map/ppermute | solution.py:458
  103.5 1.6 %collective-permute-start.26 = (bf16[48,512]{1,0:T(8,128)(2,1)S(1)}, bf16[48,512]{1,0:T(8,128)(2,1)S(1)}, u32[]{:S(2)}, u32[]{:S(2)}) collective-permute-start(bf16[48,512]{1,0:T(8,128)(2,1)S(1)} %get-tuple-element.338), channel_id=1, source_target_pairs={{0,8},{1,9},{2,10},{3,11},{4,20},{5,21},{6,22},{7,23},{8,0},{9,1},... | collective-permute-start | bytes 147464 | tf_op jit(solution)/shard_map/ppermute | solution.py:458
  105.1 2.6 %collective-permute-done.26.refs_0_ = bf16[48,512]{1,0:T(8,128)(2,1)S(1)} collective-permute-done((bf16[48,512]{1,0:T(8,128)(2,1)S(1)}, bf16[48,512]{1,0:T(8,128)(2,1)S(1)}, u32[]{:S(2)}, u32[]{:S(2)}) %collective-permute-start.26) | collective-permute-done | bytes 49184 | tf_op jit(solution)/shard_map/ppermute | solution.py:458
  107.7 2.5 %collective-permute-start.27 = (bf16[48,512]{1,0:T(8,128)(2,1)S(1)}, bf16[48,512]{1,0:T(8,128)(2,1)S(1)}, u32[]{:S(2)}, u32[]{:S(2)}) collective-permute-start(bf16[48,512]{1,0:T(8,128)(2,1)S(1)} %get-tuple-element.341.refs_1_), channel_id=1, source_target_pairs={{0,16},{1,17},{2,18},{3,19},{4,12},{5,13},{6,14},{7,15},{8,24},{9,... | collective-permute-start | bytes 147464 | tf_op jit(solution)/shard_map/ppermute | solution.py:458
  110.3 2.1 %collective-permute-done.27.refs_0_ = bf16[48,512]{1,0:T(8,128)(2,1)S(1)} collective-permute-done((bf16[48,512]{1,0:T(8,128)(2,1)S(1)}, bf16[48,512]{1,0:T(8,128)(2,1)S(1)}, u32[]{:S(2)}, u32[]{:S(2)}) %collective-permute-start.27) | collective-permute-done | bytes 49184 | tf_op jit(solution)/shard_map/ppermute | solution.py:458
  112.3 1.1 collective-permute-start.28
  113.5 2.8 %collective-permute-done.28.refs_1_ = bf16[32,512]{1,0:T(8,128)(2,1)S(1)} collective-permute-done((bf16[32,512]{1,0:T(8,128)(2,1)S(1)}, bf16[32,512]{1,0:T(8,128)(2,1)S(1)}, u32[]{:S(2)}, u32[]{:S(2)}) %collective-permute-start.28) | collective-permute-done | bytes 32800 | tf_op jit(solution)/shard_map/ppermute | solution.py:458
  116.3 1.1 collective-permute-start.29
  117.4 4.8 %collective-permute-done.29.refs_1_ = bf16[64,512]{1,0:T(8,128)(2,1)S(1)} collective-permute-done((bf16[64,512]{1,0:T(8,128)(2,1)S(1)}, bf16[64,512]{1,0:T(8,128)(2,1)S(1)}, u32[]{:S(2)}, u32[]{:S(2)}) %collective-permute-start.29) | collective-permute-done | bytes 65568 | tf_op jit(solution)/shard_map/ppermute | solution.py:458
  122.2 0.8 collective-permute-start.30
  123.0 4.2 %collective-permute-done.30.refs_1_ = bf16[128,512]{1,0:T(8,128)(2,1)S(1)} collective-permute-done((bf16[128,512]{1,0:T(8,128)(2,1)S(1)}, bf16[128,512]{1,0:T(8,128)(2,1)S(1)}, u32[]{:S(2)}, u32[]{:S(2)}) %collective-permute-start.30) | collective-permute-done | bytes 131104 | tf_op jit(solution)/shard_map/ppermute | solution.py:458
  127.3 0.1 collective-permute-start.31
  127.3 3.6 %shard_map.104.refs_2_ = bf16[512,512]{1,0:T(8,128)(2,1)S(1)} custom-call(bf16[528,512]{1,0:T(8,128)(2,1)} %get-tuple-element.312.refs_0_, bf16[4,512,512]{2,1,0:T(8,128)(2,1)} %get-tuple-element.306.refs_8_.refs_1_.refs_2_), custom_call_target="tpu_custom_call" | custom-call | flops 1342177280 | bytes 3162112 | tf_op jit(solution)/shard_map/pallas_call | solution.py:86
  131.0 2.1 %shard_map.105.refs_2_ = bf16[512,512]{1,0:T(8,128)(2,1)S(1)} custom-call(bf16[528,512]{1,0:T(8,128)(2,1)} %get-tuple-element.312.refs_0_, bf16[528,512]{1,0:T(8,128)(2,1)S(1)} %get-tuple-element.309.refs_1_, bf16[512,512]{1,0:T(8,128)(2,1)S(1)} %shard_map.104.refs_2_), custom_call_target="tpu_custom_call" | custom-call | flops 805306368 | bytes 2129920 | tf_op jit(solution)/shard_map/pallas_call | solution.py:86
  133.1 2.7 %shard_map.107.refs_3_ = bf16[512,512]{1,0:T(8,128)(2,1)S(1)} custom-call(bf16[512,512]{1,0:T(8,128)(2,1)S(1)} %get-tuple-element.317.refs_0_.refs_1_, s32[2,512]{1,0:T(2,128)S(1)} %bitcast.31, bf16[4,512,512]{2,1,0:T(8,128)(2,1)} %get-tuple-element.306.refs_8_.refs_1_.refs_2_), custom_call_target="tpu_custom_call" | custom-call | flops 1073741824 | bytes 3149824 | tf_op jit(solution)/shard_map/pallas_call | solution.py:86
  135.8 2.0 %shard_map.108 = (f32[512,512]{1,0:T(8,128)}, f32[1,512]{1,0:T(1,128)}) custom-call(f32[512,512]{1,0:T(8,128)S(1)} %get-tuple-element.307.refs_0_, f32[1,512]{1,0:T(1,128)S(1)} %get-tuple-element.308.refs_1_, bf16[512,512]{1,0:T(8,128)(2,1)S(1)} %shard_map.105.refs_2_, bf16[512,512]{1,0:T(8,128)(2,1)S(1)} %shard_map.107.refs_3_, s32[2,512]{1,0:T(2,128)S(1)} %bitcast.48), custom_call_target="tpu_custom_call" | custom-call | flops 536870912 | bytes 3153920 | tf_op jit(solution)/shard_map/pallas_call | solution.py:86
  137.8 0.5 slice.11
  139.0 1.4 spread.2.refs_2_
  140.4 0.0 collective-permute-done.22.refs_0_
  140.4 1.4 spread.3
  (20 shorter events, 0.3 us)
Async XLA Ops:
  4.6 15.2 %copy-start = (f32[1,512,512]{2,1,0:T(8,128)S(1)}, f32[1,512,512]{2,1,0:T(8,128)}, u32[]{:S(2)}) copy-start(f32[1,512,512]{2,1,0:T(8,128)} %param.21) | copy-start | bytes 3145732
  4.6 15.2 %copy-start.1 = (s32[1,1,2,512]{3,2,1,0:T(2,128)S(1)}, s32[1,1,2,512]{3,2,1,0:T(2,128)}, u32[]{:S(2)}) copy-start(s32[1,1,2,512]{3,2,1,0:T(2,128)} %param.26) | copy-start | bytes 12292
  4.6 15.2 %copy-start.2 = (f32[1,512]{1,0:T(1,128)S(1)}, f32[1,512]{1,0:T(1,128)}, u32[]{:S(2)}) copy-start(f32[1,512]{1,0:T(1,128)} %refs_3_.1) | copy-start | bytes 6148
  4.6 15.1 %collective-permute-start.2 = (bf16[528,512]{1,0:T(8,128)(2,1)S(1)}, bf16[528,512]{1,0:T(8,128)(2,1)}, u32[]{:S(2)}, u32[]{:S(2)}) collective-permute-start(bf16[528,512]{1,0:T(8,128)(2,1)S(1)} %get-tuple-element.154.refs_0_), channel_id=1, source_target_pairs={{0,12},{4,8},{8,4},{12,0},{16,28},{20,24},{24,20},{28,16},{1,13},{... | collective-permute-start | bytes 1622024 | tf_op jit(solution)/shard_map/cond/branch_2_fun/ppermute | solution.py:610
  19.8 8.5 %copy-start.3 = (s32[1,1,2,512]{3,2,1,0:T(2,128)S(1)}, s32[1,1,2,512]{3,2,1,0:T(2,128)}, u32[]{:S(2)}) copy-start(s32[1,1,2,512]{3,2,1,0:T(2,128)} %param.27) | copy-start | bytes 12292
  19.8 8.5 %copy-start.4 = (s32[1,1,2,512]{3,2,1,0:T(2,128)S(1)}, s32[1,1,2,512]{3,2,1,0:T(2,128)}, u32[]{:S(2)}) copy-start(s32[1,1,2,512]{3,2,1,0:T(2,128)} %param.25) | copy-start | bytes 12292
  19.8 8.5 %copy-start.5 = (bf16[512,512]{1,0:T(8,128)(2,1)S(1)}, bf16[512,512]{1,0:T(8,128)(2,1)}, u32[]{:S(2)}) copy-start(bf16[512,512]{1,0:T(8,128)(2,1)} %get-tuple-element.310) | copy-start | bytes 1572868
  28.4 15.7 %collective-permute-start.13 = (bf16[528,512]{1,0:T(8,128)(2,1)S(1)}, bf16[528,512]{1,0:T(8,128)(2,1)}, u32[]{:S(2)}, u32[]{:S(2)}) collective-permute-start(bf16[528,512]{1,0:T(8,128)(2,1)S(1)} %get-tuple-element.249.refs_0_), channel_id=1, source_target_pairs={{0,28},{4,24},{8,20},{12,16},{16,12},{20,8},{24,4},{28,0},{1,29},{... | collective-permute-start | bytes 1622024 | tf_op jit(solution)/shard_map/cond/branch_6_fun/ppermute | solution.py:610
  47.7 2.4 %collective-permute-start.14 = (bf16[768,512]{1,0:T(8,128)(2,1)S(1)}, bf16[768,512]{1,0:T(8,128)(2,1)S(1)}, u32[]{:S(2)}, u32[]{:S(2)}) collective-permute-start(bf16[768,512]{1,0:T(8,128)(2,1)S(1)} %get-tuple-element.320), channel_id=1, source_target_pairs={{0,4},{1,5},{2,6},{3,7},{4,0},{5,1},{6,2},{7,3},{8,12},{9,13},{10,... | collective-permute-start | bytes 2359304 | tf_op jit(solution)/shard_map/ppermute | solution.py:458
  50.3 8.0 %collective-permute-start.15 = (bf16[384,512]{1,0:T(8,128)(2,1)S(1)}, bf16[384,512]{1,0:T(8,128)(2,1)S(1)}, u32[]{:S(2)}, u32[]{:S(2)}) collective-permute-start(bf16[384,512]{1,0:T(8,128)(2,1)S(1)} %get-tuple-element.323), channel_id=1, source_target_pairs={{0,8},{1,9},{2,10},{3,11},{4,20},{5,21},{6,22},{7,23},{8,0},{9,1},... | collective-permute-start | bytes 1179656 | tf_op jit(solution)/shard_map/ppermute | solution.py:458
  58.5 5.7 %collective-permute-start.16 = (bf16[192,512]{1,0:T(8,128)(2,1)S(1)}, bf16[192,512]{1,0:T(8,128)(2,1)S(1)}, u32[]{:S(2)}, u32[]{:S(2)}) collective-permute-start(bf16[192,512]{1,0:T(8,128)(2,1)S(1)} %get-tuple-element.325), channel_id=1, source_target_pairs={{0,16},{1,17},{2,18},{3,19},{4,12},{5,13},{6,14},{7,15},{8,24},{9,... | collective-permute-start | bytes 589832 | tf_op jit(solution)/shard_map/ppermute | solution.py:458
  64.2 4.7 %collective-permute-start.17 = (bf16[96,512]{1,0:T(8,128)(2,1)S(1)}, bf16[96,512]{1,0:T(8,128)(2,1)S(1)}, u32[]{:S(2)}, u32[]{:S(2)}) collective-permute-start(bf16[96,512]{1,0:T(8,128)(2,1)S(1)} %get-tuple-element.327), channel_id=1, source_target_pairs={{0,1},{1,0},{2,3},{3,2},{4,5},{5,4},{6,7},{7,6},{8,9},{9,8},{10,11... | collective-permute-start | bytes 294920 | tf_op jit(solution)/shard_map/ppermute | solution.py:458
  69.0 6.3 %collective-permute-start.18 = (bf16[96,512]{1,0:T(8,128)(2,1)S(1)}, bf16[96,512]{1,0:T(8,128)(2,1)S(1)}, u32[]{:S(2)}, u32[]{:S(2)}) collective-permute-start(bf16[96,512]{1,0:T(8,128)(2,1)S(1)} %shard_map.113.refs_1_), channel_id=1, source_target_pairs={{0,2},{1,3},{2,0},{3,1},{4,6},{5,7},{6,4},{7,5},{8,10},{9,11},{10,... | collective-permute-start | bytes 294920 | tf_op jit(solution)/shard_map/ppermute | solution.py:458
  75.3 4.7 %collective-permute-start.19 = (bf16[96,512]{1,0:T(8,128)(2,1)S(1)}, bf16[96,512]{1,0:T(8,128)(2,1)S(1)}, u32[]{:S(2)}, u32[]{:S(2)}) collective-permute-start(bf16[96,512]{1,0:T(8,128)(2,1)S(1)} %shard_map.114.refs_0_), channel_id=1, source_target_pairs={{0,1},{1,0},{2,3},{3,2},{4,5},{5,4},{6,7},{7,6},{8,9},{9,8},{10,11... | collective-permute-start | bytes 294920 | tf_op jit(solution)/shard_map/ppermute | solution.py:458
  80.0 7.0 %collective-permute-start.20 = (bf16[192,512]{1,0:T(8,128)(2,1)S(1)}, bf16[192,512]{1,0:T(8,128)(2,1)S(1)}, u32[]{:S(2)}, u32[]{:S(2)}) collective-permute-start(bf16[192,512]{1,0:T(8,128)(2,1)S(1)} %shard_map.115.refs_0_), channel_id=1, source_target_pairs={{0,16},{1,17},{2,18},{3,19},{4,12},{5,13},{6,14},{7,15},{8,24},{9,... | collective-permute-start | bytes 589832 | tf_op jit(solution)/shard_map/ppermute | solution.py:458
  81.8 6.9 %collective-permute-start.23 = (bf16[272,512]{1,0:T(8,128)(2,1)S(1)}, bf16[272,512]{1,0:T(8,128)(2,1)S(1)}, u32[]{:S(2)}, u32[]{:S(2)}) collective-permute-start(bf16[272,512]{1,0:T(8,128)(2,1)S(1)} %get-tuple-element.329), channel_id=1, source_target_pairs={{0,4},{1,5},{2,6},{3,7},{4,0},{5,1},{6,2},{7,3},{8,12},{9,13},{10,... | collective-permute-start | bytes 835592 | tf_op jit(solution)/shard_map/ppermute | solution.py:458
  87.1 7.8 %collective-permute-start.21 = (bf16[384,512]{1,0:T(8,128)(2,1)S(1)}, bf16[384,512]{1,0:T(8,128)(2,1)S(1)}, u32[]{:S(2)}, u32[]{:S(2)}) collective-permute-start(bf16[384,512]{1,0:T(8,128)(2,1)S(1)} %shard_map.116.refs_0_), channel_id=1, source_target_pairs={{0,8},{1,9},{2,10},{3,11},{4,20},{5,21},{6,22},{7,23},{8,0},{9,1},... | collective-permute-start | bytes 1179656 | tf_op jit(solution)/shard_map/ppermute | solution.py:458
  88.8 6.3 %collective-permute-start.24 = (bf16[144,512]{1,0:T(8,128)(2,1)S(1)}, bf16[144,512]{1,0:T(8,128)(2,1)S(1)}, u32[]{:S(2)}, u32[]{:S(2)}) collective-permute-start(bf16[144,512]{1,0:T(8,128)(2,1)S(1)} %get-tuple-element.332), channel_id=1, source_target_pairs={{0,1},{1,0},{2,3},{3,2},{4,5},{5,4},{6,7},{7,6},{8,9},{9,8},{10,11... | collective-permute-start | bytes 442376 | tf_op jit(solution)/shard_map/ppermute | solution.py:458
  95.1 45.3 %collective-permute-start.22 = (bf16[768,512]{1,0:T(8,128)(2,1)S(1)}, bf16[768,512]{1,0:T(8,128)(2,1)S(1)}, u32[]{:S(2)}, u32[]{:S(2)}) collective-permute-start(bf16[768,512]{1,0:T(8,128)(2,1)S(1)} %shard_map.117.refs_0_), channel_id=1, source_target_pairs={{0,4},{1,5},{2,6},{3,7},{4,0},{5,1},{6,2},{7,3},{8,12},{9,13},{10,... | collective-permute-start | bytes 2359304 | tf_op jit(solution)/shard_map/ppermute | solution.py:458
  95.2 8.3 %collective-permute-start.25 = (bf16[80,512]{1,0:T(8,128)(2,1)S(1)}, bf16[80,512]{1,0:T(8,128)(2,1)S(1)}, u32[]{:S(2)}, u32[]{:S(2)}) collective-permute-start(bf16[80,512]{1,0:T(8,128)(2,1)S(1)} %get-tuple-element.335), channel_id=1, source_target_pairs={{0,2},{1,3},{2,0},{3,1},{4,6},{5,7},{6,4},{7,5},{8,10},{9,11},{10,... | collective-permute-start | bytes 245768 | tf_op jit(solution)/shard_map/ppermute | solution.py:458
  103.5 4.2 %collective-permute-start.26 = (bf16[48,512]{1,0:T(8,128)(2,1)S(1)}, bf16[48,512]{1,0:T(8,128)(2,1)S(1)}, u32[]{:S(2)}, u32[]{:S(2)}) collective-permute-start(bf16[48,512]{1,0:T(8,128)(2,1)S(1)} %get-tuple-element.338), channel_id=1, source_target_pairs={{0,8},{1,9},{2,10},{3,11},{4,20},{5,21},{6,22},{7,23},{8,0},{9,1},... | collective-permute-start | bytes 147464 | tf_op jit(solution)/shard_map/ppermute | solution.py:458
  107.7 4.6 %collective-permute-start.27 = (bf16[48,512]{1,0:T(8,128)(2,1)S(1)}, bf16[48,512]{1,0:T(8,128)(2,1)S(1)}, u32[]{:S(2)}, u32[]{:S(2)}) collective-permute-start(bf16[48,512]{1,0:T(8,128)(2,1)S(1)} %get-tuple-element.341.refs_1_), channel_id=1, source_target_pairs={{0,16},{1,17},{2,18},{3,19},{4,12},{5,13},{6,14},{7,15},{8,24},{9,... | collective-permute-start | bytes 147464 | tf_op jit(solution)/shard_map/ppermute | solution.py:458
  112.3 4.0 %collective-permute-start.28 = (bf16[32,512]{1,0:T(8,128)(2,1)S(1)}, bf16[32,512]{1,0:T(8,128)(2,1)S(1)}, u32[]{:S(2)}, u32[]{:S(2)}) collective-permute-start(bf16[32,512]{1,0:T(8,128)(2,1)S(1)} %get-tuple-element.343.refs_0_), channel_id=1, source_target_pairs={{0,8},{1,9},{2,10},{3,11},{4,20},{5,21},{6,22},{7,23},{8,0},{9,1},... | collective-permute-start | bytes 98312 | tf_op jit(solution)/shard_map/ppermute | solution.py:458
  116.3 5.8 %collective-permute-start.29 = (bf16[64,512]{1,0:T(8,128)(2,1)S(1)}, bf16[64,512]{1,0:T(8,128)(2,1)S(1)}, u32[]{:S(2)}, u32[]{:S(2)}) collective-permute-start(bf16[64,512]{1,0:T(8,128)(2,1)S(1)} %shard_map.123.refs_0_), channel_id=1, source_target_pairs={{0,2},{1,3},{2,0},{3,1},{4,6},{5,7},{6,4},{7,5},{8,10},{9,11},{10,... | collective-permute-start | bytes 196616 | tf_op jit(solution)/shard_map/ppermute | solution.py:458
  122.2 5.0 %collective-permute-start.30 = (bf16[128,512]{1,0:T(8,128)(2,1)S(1)}, bf16[128,512]{1,0:T(8,128)(2,1)S(1)}, u32[]{:S(2)}, u32[]{:S(2)}) collective-permute-start(bf16[128,512]{1,0:T(8,128)(2,1)S(1)} %shard_map.124.refs_0_), channel_id=1, source_target_pairs={{0,1},{1,0},{2,3},{3,2},{4,5},{5,4},{6,7},{7,6},{8,9},{9,8},{10,11... | collective-permute-start | bytes 393224 | tf_op jit(solution)/shard_map/ppermute | solution.py:458
  127.3 13.1 %collective-permute-start.31 = (bf16[256,512]{1,0:T(8,128)(2,1)S(1)}, bf16[256,512]{1,0:T(8,128)(2,1)S(1)}, u32[]{:S(2)}, u32[]{:S(2)}) collective-permute-start(bf16[256,512]{1,0:T(8,128)(2,1)S(1)} %shard_map.125.refs_1_), channel_id=1, source_target_pairs={{0,4},{1,5},{2,6},{3,7},{4,0},{5,1},{6,2},{7,3},{8,12},{9,13},{10,... | collective-permute-start | bytes 786440 | tf_op jit(solution)/shard_map/ppermute | solution.py:458
